TPU v7x, 32 devices: a whole 2x2x4 slice. The times are simulated.
32 devices in a mesh: slab: 4 (over x, core), dom: 8 (over z, y).
Axes of the slice: x: 2, y: 2, z: 4, core: 2. Of those that a mesh axis runs over, the one named last changes fastest.
Arguments:
- donors: bfloat16 [262144, 128], P(('slab', 'dom')), may hold values from -6 to 6
- send_block: int32 [4, 8, 8, 8], P('slab', 'dom'), may hold values from 0 to 63
- send_count: int32 [4, 8, 8], P('slab', 'dom'), may hold values from 1 to 8, as said below
- send_target: int32 [4, 8, 8, 8], P('slab', 'dom'), may hold values from 0 to 1
- target_block: int32 [4, 8, 8, 2], P('slab', 'dom'), may hold values from 0 to 7
- weights: bfloat16 [4, 8, 8, 8, 128, 128], P('slab', 'dom'), may hold values from -0.25 to 0.25
- halo_weights: bfloat16 [4, 8, 2, 128, 128], P('slab', 'dom'), may hold values from -0.375 to 0.375
- permute: int32 [4, 8, 1024], P('slab', 'dom'), may hold values from 0 to 1023, each once within a row
Outputs:
- balanced: bfloat16 [32768, 128], P(('slab', 'dom'))
Inputs may be any that keep to these rules, and one draw needn't show every extreme that they name: `send_count`: each source has at least one destination with exactly 8 live slots.
All inputs are finite; a program needn't handle non-finite values.
Results may differ from a plain program's by a relative error of at most 0.0047.
Values may be sent and summed in bfloat16 or wider, within the bound.
No kernel may reach another device: no remote copies, remote signals or barrier semaphores. Data moves between devices by JAX's collectives and lax.ppermute only.
A program may use at most 128 MiB of HBM per device.

v0:
```python
import functools

import jax
import jax.numpy as jnp
from jax import lax
from jax.experimental import pallas as pl
from jax.experimental.pallas import tpu as pltpu
from jax.sharding import PartitionSpec as P


VMEM = pl.BlockSpec(memory_space=pltpu.VMEM)
SMEM = pl.BlockSpec(memory_space=pltpu.SMEM)
HBM = pl.BlockSpec(memory_space=pltpu.HBM)
MARGIN = 4 << 20


def nbytes(*arrays):
    return sum(a.size * jnp.dtype(a.dtype).itemsize for a in arrays)


def swap(value, step):
    count = lax.axis_size("dom")
    return lax.ppermute(value, "dom", [(source, source ^ step) for source in range(count)])


def parts_kernel(steps, load, *refs):
    block_hbm, count_hbm, target_hbm, donors, weights = refs[:5]
    outs = refs[5 : 5 + len(steps)]
    extra = refs[5 + len(steps)]
    held_d = extra if load else donors
    block_of, count_of, target_of, held_w, sems, sem_w = refs[-6:]
    rows = held_w.shape[2]
    capacity = held_w.shape[1]
    width = held_d.shape[1]
    half = block_of.shape[0] // 2
    places = outs[0].shape[0] // (2 * rows)
    me = lax.axis_index("dom")
    owners = []
    for step in steps:
        owners += [jnp.bitwise_xor(me, step), jnp.bitwise_xor(me, step + half)]
    tables = [
        pltpu.make_async_copy(block_hbm, block_of, sems.at[0]),
        pltpu.make_async_copy(count_hbm, count_of, sems.at[1]),
        pltpu.make_async_copy(target_hbm, target_of, sems.at[2]),
    ]
    if load:
        tables.append(pltpu.make_async_copy(donors, held_d, sems.at[3]))
    loads = [
        pltpu.make_async_copy(weights.at[p], held_w.at[i], sem_w.at[i])
        for i, p in enumerate(owners)
    ]
    for copy in tables + loads:
        copy.start()
    for copy in tables:
        copy.wait()
    for i, p in enumerate(owners):
        loads[i].wait()
        total = None
        for c in range(0, capacity, 2):
            left = jnp.concatenate([held_w[i, c], held_w[i, c + 1]], axis=1)
            pieces = []
            for k in (c, c + 1):
                row = pl.multiple_of(block_of[p, k] * rows, rows)
                block = held_d[pl.ds(row, rows)]
                live = k < count_of[p]
                kept = []
                for t in range(places):
                    wanted = jnp.logical_and(live, target_of[p, k] == t)
                    kept.append(jnp.where(wanted, block, jnp.zeros_like(block)))
                pieces.append(jnp.concatenate(kept, axis=1))
            right = jnp.concatenate(pieces, axis=0)
            prod = jnp.dot(left, right, preferred_element_type=jnp.float32)
            total = prod if total is None else total + prod
        for t in range(places):
            at = ((i % 2) * places + t) * rows
            outs[i // 2][at : at + rows] = total[:, t * width : (t + 1) * width].astype(
                outs[0].dtype
            )
    if not load:
        extra[...] = held_d[held_d.shape[0] - extra.shape[0] : held_d.shape[0]]


def form_parts(steps, tables, donors, weights, places, load, extra_rows):
    _, capacity, rows, _ = weights.shape
    width = donors.shape[1]
    shapes = [jax.ShapeDtypeStruct((2 * places * rows, width), jnp.bfloat16)] * len(steps)
    shapes.append(jax.ShapeDtypeStruct((extra_rows, width), donors.dtype))
    in_hbm = functools.partial(pltpu.with_memory_space_constraint, memory_space=pltpu.HBM)
    held = jax.ShapeDtypeStruct((2 * len(steps), capacity, rows, rows), weights.dtype)
    return pl.pallas_call(
        functools.partial(parts_kernel, steps, load),
        out_shape=shapes,
        in_specs=[HBM, HBM, HBM, HBM if load else VMEM, HBM],
        out_specs=[VMEM] * len(shapes),
        scratch_shapes=[pltpu.SMEM(table.shape, table.dtype) for table in tables]
        + [
            pltpu.VMEM(held.shape, held.dtype),
            pltpu.SemaphoreType.DMA((4,)),
            pltpu.SemaphoreType.DMA((2 * len(steps),)),
        ],
        compiler_params=pltpu.CompilerParams(
            vmem_limit_bytes=nbytes(held, donors, *shapes) + MARGIN
        ),
        cost_estimate=pl.CostEstimate(
            flops=8 * len(steps) * capacity * rows * rows * width,
            bytes_accessed=nbytes(held, donors),
            transcendentals=0,
        ),
        name="parts",
    )(*map(in_hbm, tables), in_hbm(donors) if load else donors, in_hbm(weights))


def choose_kernel(steps, with_halo, place_of, order, *refs):
    halo_w = refs[0] if with_halo else None
    chosen = refs[-1]
    rows = order.shape[1]
    places = place_of.shape[0]
    me = lax.axis_index("dom")
    lane = lax.broadcasted_iota(jnp.int32, (rows, rows), 1)
    starts = []
    for step in steps:
        q = jnp.bitwise_xor(me, step)
        starts += [place_of[t, q] * rows for t in range(places)]

    def fill(j, carry):
        wanted = jnp.broadcast_to(order[pl.ds(j, 1), :], (rows, rows)).T - lane
        row = pl.multiple_of(j * rows, rows)
        for b, begin in enumerate(starts):
            chosen[pl.ds(row, rows), b * rows : (b + 1) * rows] = jnp.where(
                wanted == begin, 1.0, 0.0
            ).astype(jnp.bfloat16)
        if with_halo:
            first = jnp.where(wanted == 0, 1.0, 0.0).astype(jnp.bfloat16)
            for h in range(halo_w.shape[0]):
                at = (len(starts) + h) * rows
                chosen[pl.ds(row, rows), at : at + rows] = jnp.dot(
                    first, halo_w[h], preferred_element_type=jnp.float32
                ).astype(jnp.bfloat16)
        return carry

    lax.fori_loop(0, order.shape[0], fill, 0)


def choose(steps, place_of, order, halo_w=None):
    extra = [] if halo_w is None else [halo_w]
    columns = len(steps) * place_of.shape[0] * order.shape[1]
    columns += sum(h.shape[0] * h.shape[1] for h in extra)
    shape = jax.ShapeDtypeStruct((order.size, columns), jnp.bfloat16)
    return pl.pallas_call(
        functools.partial(choose_kernel, steps, bool(extra)),
        out_shape=shape,
        in_specs=[SMEM, VMEM] + [VMEM] * len(extra),
        out_specs=VMEM,
        compiler_params=pltpu.CompilerParams(
            vmem_limit_bytes=nbytes(order, shape, *extra) + MARGIN
        ),
        cost_estimate=pl.CostEstimate(
            flops=shape.size, bytes_accessed=nbytes(shape), transcendentals=0
        ),
        name="choose",
    )(place_of, order, *extra)


def place_kernel(steps, far, share, own, other, rim, *refs):
    outs = refs[-1 - len(steps) : -1]
    parts = refs[: -1 - len(steps)]
    rows_of = refs[-1]
    me = lax.axis_index("dom")
    lot = len(steps) * share
    half = len(steps)
    begin = jnp.bitwise_xor(me // half, 1 if far else 0) * lot
    begin = pl.multiple_of(begin, lot)
    depth = parts[0].shape[0] // 2
    for side, matrix in enumerate((own, other)):
        total = None
        for i, part in enumerate(parts):
            prod = jnp.dot(
                matrix[pl.ds(begin, lot), i * depth : (i + 1) * depth],
                part[side * depth : (side + 1) * depth],
                preferred_element_type=jnp.float32,
            )
            total = prod if total is None else total + prod
        if side == 0:
            total += jnp.dot(
                matrix[pl.ds(begin, lot), len(parts) * depth :],
                rim[...],
                preferred_element_type=jnp.float32,
            )
        rows_of[side] = total
    for step, out in zip(steps, outs):
        at = pl.multiple_of(lax.rem(jnp.bitwise_xor(me, step), half) * share, share)
        for side in range(2):
            out[side * share : (side + 1) * share] = rows_of[side, pl.ds(at, share)].astype(
                out.dtype
            )


def place(steps, far, share, own, other, rim, parts):
    width = rim.shape[1]
    shapes = [jax.ShapeDtypeStruct((2 * share, width), jnp.bfloat16)] * len(steps)
    held = jax.ShapeDtypeStruct((2, len(steps) * share, width), jnp.float32)
    return pl.pallas_call(
        functools.partial(place_kernel, steps, far, share),
        out_shape=shapes,
        in_specs=[VMEM] * (3 + len(parts)),
        out_specs=[VMEM] * len(shapes),
        scratch_shapes=[pltpu.VMEM(held.shape, held.dtype)],
        compiler_params=pltpu.CompilerParams(
            vmem_limit_bytes=nbytes(own, other, rim, held, *parts, *shapes) + MARGIN
        ),
        cost_estimate=pl.CostEstimate(
            flops=own.size * width * 2, bytes_accessed=nbytes(own), transcendentals=0
        ),
        name="place",
    )(own, other, rim, *parts)


def join_kernel(count, *refs):
    chunks = refs[:count]
    out, held, sem = refs[count:]
    share = chunks[0].shape[0] // 2
    me = lax.axis_index("dom")
    copies = []
    for step in range(count):
        row = pl.multiple_of(jnp.bitwise_xor(me, step) * share, share)
        pair = chunks[step ^ (count // 2)]
        total = chunks[step][:share].astype(jnp.float32) + pair[share:].astype(jnp.float32)
        held[step] = total.astype(held.dtype)
        copies.append(pltpu.make_async_copy(held.at[step], out.at[pl.ds(row, share)], sem.at[step]))
        copies[-1].start()
    for copy in copies:
        copy.wait()


def join(chunks):
    count = len(chunks)
    share, width = chunks[0].shape[0] // 2, chunks[0].shape[1]
    return pl.pallas_call(
        functools.partial(join_kernel, count),
        out_shape=jax.ShapeDtypeStruct((share * count, width), chunks[0].dtype),
        in_specs=[VMEM] * count,
        out_specs=HBM,
        scratch_shapes=[
            pltpu.VMEM((count, share, width), chunks[0].dtype),
            pltpu.SemaphoreType.DMA((count,)),
        ],
        compiler_params=pltpu.CompilerParams(vmem_limit_bytes=2 * nbytes(*chunks) + MARGIN),
        name="join",
    )(*chunks)


def on_device(
    donors, send_block, send_count, send_target, target_block, weights, halo_weights, permute
):
    block_rows = weights.shape[-1]
    rim_rows = halo_weights.shape[2] * block_rows
    count = lax.axis_size("dom")
    slabs = lax.axis_size("slab")
    half = count // 2
    share = permute.shape[-1] // count
    tables = send_block[0, 0], send_count[0, 0], send_target[0, 0]
    places = target_block.shape[-1]
    form = functools.partial(form_parts, tables=tables, weights=weights[0, 0], places=places)
    near = list(range(1, half))
    *first, held = form(near[:1], donors=donors, load=True, extra_rows=donors.shape[0])
    *second, rim = form(near[1:] + [0], donors=held, load=False, extra_rows=rim_rows)
    own_part = second.pop()
    arrived = [swap(part, step) for part, step in zip(first + second, near)]
    order = permute[0, 0].reshape(-1, block_rows)
    other_order = swap(order, half)
    table = target_block[0, 0].T
    other_table = swap(table, half)
    rim = lax.ppermute(rim, "slab", [(source, source + 1) for source in range(slabs - 1)])
    own = choose([0] + near, table, order, halo_weights[0, 0])
    other = choose([0] + near, other_table, other_order)
    parts = [own_part] + arrived
    far_steps = list(range(count - 1, half - 1, -1))
    far = place(far_steps, True, share, own, other, rim, parts)
    close_steps = list(range(half - 1, -1, -1))
    close = place(close_steps, False, share, own, other, rim, parts)
    chunks = [None] * count
    chunks[0] = close[-1]
    for step, chunk in zip(far_steps + close_steps[:-1], far + close[:-1]):
        chunks[step] = swap(chunk, step)
    return join(chunks)


def solution(mesh):
    return jax.shard_map(
        on_device,
        mesh=mesh,
        in_specs=(
            P(("slab", "dom"), None),
            P("slab", "dom", None, None),
            P("slab", "dom", None),
            P("slab", "dom", None, None),
            P("slab", "dom", None, None),
            P("slab", "dom", None, None, None, None),
            P("slab", "dom", None, None, None),
            P("slab", "dom", None),
        ),
        out_specs=P(("slab", "dom"), None),
        check_vma=False,
    )
```

profile of v0, /device:TPU:0, one launch (start us, length us, event | category | flops | bytes accessed | tf_op | source)
XLA Modules:
  0.0 42.8 jit_solution(14393070718829174857)
XLA Ops:
  0.0 2.2 %parts.2 = (bf16[512,128]{1,0:T(8,128)(2,1)S(1)}, bf16[8192,128]{1,0:T(8,128)(2,1)S(1)}) custom-call(s32[8,8]{1,0:T(8,128)} %bitcast.16, s32[8]{0:T(128)} %bitcast.20, s32[8,8]{1,0:T(8,128)} %bitcast.18, bf16[8192,128]{1,0:T(8,128)(2,1)} %refs_3_.1, bf16[8,8,128,128]{3,2,1,0:T(8,128)(2,1)} %bitcast.14), custom_call_target="tpu_custom_call" | custom-call | flops 134217728 | bytes 2621440 | tf_op jit(solution)/shard_map/parts/pallas_call | solution.py:90
  2.2 0.0 copy-start.2
  2.3 2.8 %parts.3 = (bf16[512,128]{1,0:T(8,128)(2,1)S(1)}, bf16[512,128]{1,0:T(8,128)(2,1)S(1)}, bf16[512,128]{1,0:T(8,128)(2,1)S(1)}, bf16[256,128]{1,0:T(8,128)(2,1)S(1)}) custom-call(s32[8,8]{1,0:T(8,128)} %bitcast.17, s32[8]{0:T(128)} %bitcast.21, s32[8,8]{1,0:T(8,128)} %bitcast.19, bf16[8192,128]{1,0:T(8,128)(2,1)S(1)} %get-tuple-element.19.refs_3_, ...), custom_call_target="tpu_custom_call" | custom-call | flops 402653184 | bytes 3670016 | tf_op jit(solution)/shard_map/parts/pallas_call | solution.py:90
  5.1 3.1 %collective-permute-start.4 = (bf16[512,128]{1,0:T(8,128)(2,1)S(1)}, bf16[512,128]{1,0:T(8,128)(2,1)S(1)}, u32[]{:S(2)}, u32[]{:S(2)}) collective-permute-start(bf16[512,128]{1,0:T(8,128)(2,1)S(1)} %get-tuple-element.23), channel_id=1, source_target_pairs={{0,2},{1,3},{2,0},{3,1},{4,6},{5,7},{6,4},{7,5},{8,10},{9,11},{10,... | collective-permute-start | bytes 393224 | tf_op jit(solution)/shard_map/ppermute | solution.py:23
  8.2 1.4 %collective-permute-start.5 = (bf16[512,128]{1,0:T(8,128)(2,1)S(1)}, bf16[512,128]{1,0:T(8,128)(2,1)S(1)}, u32[]{:S(2)}, u32[]{:S(2)}) collective-permute-start(bf16[512,128]{1,0:T(8,128)(2,1)S(1)} %get-tuple-element.24), channel_id=1, source_target_pairs={{0,3},{1,2},{2,1},{3,0},{4,7},{5,6},{6,5},{7,4},{8,11},{9,10},{10,... | collective-permute-start | bytes 393224 | tf_op jit(solution)/shard_map/ppermute | solution.py:23
  9.6 0.1 collective-permute-start.3
  9.8 1.3 %collective-permute-start.2 = (bf16[256,128]{1,0:T(8,128)(2,1)S(1)}, bf16[256,128]{1,0:T(8,128)(2,1)S(1)}, u32[]{:S(2)}, u32[]{:S(2)}) collective-permute-start(bf16[256,128]{1,0:T(8,128)(2,1)S(1)} %get-tuple-element.20), channel_id=1, source_target_pairs={{0,8},{8,16},{16,24},{1,9},{9,17},{17,25},{2,10},{10,18},{18,26},{... | collective-permute-start | bytes 196616 | tf_op jit(solution)/shard_map/ppermute | solution.py:273
  11.1 3.0 %collective-permute-start = (s32[2,8]{1,0:T(2,128)S(1)}, s32[2,8]{1,0:T(2,128)S(1)}, u32[]{:S(2)}, u32[]{:S(2)}) collective-permute-start(s32[2,8]{1,0:T(2,128)S(1)} %bitcast.12), channel_id=1, source_target_pairs={{0,4},{1,5},{2,6},{3,7},{4,0},{5,1},{6,2},{7,3},{8,12},{9,13},{10,... | collective-permute-start | bytes 200 | tf_op jit(solution)/shard_map/ppermute | solution.py:23
  14.1 1.6 %collective-permute-done.place_of = s32[2,8]{1,0:T(2,128)S(1)} collective-permute-done((s32[2,8]{1,0:T(2,128)S(1)}, s32[2,8]{1,0:T(2,128)S(1)}, u32[]{:S(2)}, u32[]{:S(2)}) %collective-permute-start) | collective-permute-done | bytes 96 | tf_op jit(solution)/shard_map/ppermute | solution.py:23
  15.7 2.9 %collective-permute-start.1 = (s32[8,128]{1,0:T(8,128)S(1)}, s32[8,128]{1,0:T(8,128)S(1)}, u32[]{:S(2)}, u32[]{:S(2)}) collective-permute-start(s32[8,128]{1,0:T(8,128)S(1)} %bitcast.10), channel_id=1, source_target_pairs={{0,4},{1,5},{2,6},{3,7},{4,0},{5,1},{6,2},{7,3},{8,12},{9,13},{10,... | collective-permute-start | bytes 12296 | tf_op jit(solution)/shard_map/ppermute | solution.py:23
  18.6 2.5 %choose.2.own = bf16[1024,1280]{1,0:T(8,128)(2,1)S(1)} custom-call(s32[2,8]{1,0:T(2,128)S(1)} %bitcast.13, s32[8,128]{1,0:T(8,128)S(1)} %bitcast.11, bf16[2,128,128]{2,1,0:T(8,128)(2,1)S(1)} %bitcast.9), custom_call_target="tpu_custom_call" | custom-call | flops 1310720 | bytes 2621440 | tf_op jit(solution)/shard_map/choose/pallas_call | solution.py:149
  21.1 1.6 %choose.3.other = bf16[1024,1024]{1,0:T(8,128)(2,1)S(1)} custom-call(s32[2,8]{1,0:T(2,128)S(1)} %collective-permute-done.place_of, s32[8,128]{1,0:T(8,128)S(1)} %collective-permute-done.1.order), custom_call_target="tpu_custom_call" | custom-call | flops 1048576 | bytes 2097152 | tf_op jit(solution)/shard_map/choose/pallas_call | solution.py:149
  22.7 0.8 %place.3 = (bf16[256,128]{1,0:T(8,128)(2,1)S(1)}, bf16[256,128]{1,0:T(8,128)(2,1)S(1)}, bf16[256,128]{1,0:T(8,128)(2,1)S(1)}, bf16[256,128]{1,0:T(8,128)(2,1)S(1)}) custom-call(bf16[1024,1280]{1,0:T(8,128)(2,1)S(1)} %choose.2.own, bf16[1024,1024]{1,0:T(8,128)(2,1)S(1)} %choose.3.other, bf16[256,128]{1,0:T(8,128)(2,1)S(1)} %collective-permute-done.2.rim, ...), custom_call_target="tpu_custom_call" | custom-call | flops 335544320 | bytes 2621440 | tf_op jit(solution)/shard_map/place/pallas_call | solution.py:202
  23.6 3.0 %collective-permute-start.10 = (bf16[256,128]{1,0:T(8,128)(2,1)S(1)}, bf16[256,128]{1,0:T(8,128)(2,1)S(1)}, u32[]{:S(2)}, u32[]{:S(2)}) collective-permute-start(bf16[256,128]{1,0:T(8,128)(2,1)S(1)} %get-tuple-element.30), channel_id=1, source_target_pairs={{0,5},{1,4},{2,7},{3,6},{4,1},{5,0},{6,3},{7,2},{8,13},{9,12},{10,... | collective-permute-start | bytes 196616 | tf_op jit(solution)/shard_map/ppermute | solution.py:23
  26.5 2.0 %collective-permute-start.11 = (bf16[256,128]{1,0:T(8,128)(2,1)S(1)}, bf16[256,128]{1,0:T(8,128)(2,1)S(1)}, u32[]{:S(2)}, u32[]{:S(2)}) collective-permute-start(bf16[256,128]{1,0:T(8,128)(2,1)S(1)} %get-tuple-element.31), channel_id=1, source_target_pairs={{0,6},{1,7},{2,4},{3,5},{4,2},{5,3},{6,0},{7,1},{8,14},{9,15},{10,... | collective-permute-start | bytes 196616 | tf_op jit(solution)/shard_map/ppermute | solution.py:23
  28.5 1.8 %collective-permute-start.12 = (bf16[256,128]{1,0:T(8,128)(2,1)S(1)}, bf16[256,128]{1,0:T(8,128)(2,1)S(1)}, u32[]{:S(2)}, u32[]{:S(2)}) collective-permute-start(bf16[256,128]{1,0:T(8,128)(2,1)S(1)} %get-tuple-element.32), channel_id=1, source_target_pairs={{0,7},{1,6},{2,5},{3,4},{4,3},{5,2},{6,1},{7,0},{8,15},{9,14},{10,... | collective-permute-start | bytes 196616 | tf_op jit(solution)/shard_map/ppermute | solution.py:23
  30.3 0.8 %place.2 = (bf16[256,128]{1,0:T(8,128)(2,1)S(1)}, bf16[256,128]{1,0:T(8,128)(2,1)S(1)}, bf16[256,128]{1,0:T(8,128)(2,1)S(1)}, bf16[256,128]{1,0:T(8,128)(2,1)S(1)}) custom-call(bf16[1024,1280]{1,0:T(8,128)(2,1)S(1)} %choose.2.own, bf16[1024,1024]{1,0:T(8,128)(2,1)S(1)} %choose.3.other, bf16[256,128]{1,0:T(8,128)(2,1)S(1)} %collective-permute-done.2.rim, ...), custom_call_target="tpu_custom_call" | custom-call | flops 335544320 | bytes 2621440 | tf_op jit(solution)/shard_map/place/pallas_call | solution.py:202
  31.1 1.6 %collective-permute-start.6 = (bf16[256,128]{1,0:T(8,128)(2,1)S(1)}, bf16[256,128]{1,0:T(8,128)(2,1)S(1)}, u32[]{:S(2)}, u32[]{:S(2)}) collective-permute-start(bf16[256,128]{1,0:T(8,128)(2,1)S(1)} %get-tuple-element.26), channel_id=1, source_target_pairs={{0,1},{1,0},{2,3},{3,2},{4,5},{5,4},{6,7},{7,6},{8,9},{9,8},{10,11... | collective-permute-start | bytes 196616 | tf_op jit(solution)/shard_map/ppermute | solution.py:23
  32.7 0.5 %collective-permute-done.10.refs_5_ = bf16[256,128]{1,0:T(8,128)(2,1)S(1)} collective-permute-done((bf16[256,128]{1,0:T(8,128)(2,1)S(1)}, bf16[256,128]{1,0:T(8,128)(2,1)S(1)}, u32[]{:S(2)}, u32[]{:S(2)}) %collective-permute-start.10) | collective-permute-done | bytes 65568 | tf_op jit(solution)/shard_map/ppermute | solution.py:23
  33.2 2.1 %collective-permute-start.7 = (bf16[256,128]{1,0:T(8,128)(2,1)S(1)}, bf16[256,128]{1,0:T(8,128)(2,1)S(1)}, u32[]{:S(2)}, u32[]{:S(2)}) collective-permute-start(bf16[256,128]{1,0:T(8,128)(2,1)S(1)} %get-tuple-element.27), channel_id=1, source_target_pairs={{0,2},{1,3},{2,0},{3,1},{4,6},{5,7},{6,4},{7,5},{8,10},{9,11},{10,... | collective-permute-start | bytes 196616 | tf_op jit(solution)/shard_map/ppermute | solution.py:23
  35.3 3.7 %collective-permute-start.8 = (bf16[256,128]{1,0:T(8,128)(2,1)S(1)}, bf16[256,128]{1,0:T(8,128)(2,1)S(1)}, u32[]{:S(2)}, u32[]{:S(2)}) collective-permute-start(bf16[256,128]{1,0:T(8,128)(2,1)S(1)} %get-tuple-element.28), channel_id=1, source_target_pairs={{0,3},{1,2},{2,1},{3,0},{4,7},{5,6},{6,5},{7,4},{8,11},{9,10},{10,... | collective-permute-start | bytes 196616 | tf_op jit(solution)/shard_map/ppermute | solution.py:23
  39.0 1.2 %collective-permute-done.9.refs_4_ = bf16[256,128]{1,0:T(8,128)(2,1)S(1)} collective-permute-done((bf16[256,128]{1,0:T(8,128)(2,1)S(1)}, bf16[256,128]{1,0:T(8,128)(2,1)S(1)}, u32[]{:S(2)}, u32[]{:S(2)}) %collective-permute-start.9) | collective-permute-done | bytes 65568 | tf_op jit(solution)/shard_map/ppermute | solution.py:23
  40.3 1.8 %collective-permute-done.8.refs_3_ = bf16[256,128]{1,0:T(8,128)(2,1)S(1)} collective-permute-done((bf16[256,128]{1,0:T(8,128)(2,1)S(1)}, bf16[256,128]{1,0:T(8,128)(2,1)S(1)}, u32[]{:S(2)}, u32[]{:S(2)}) %collective-permute-start.8) | collective-permute-done | bytes 65568 | tf_op jit(solution)/shard_map/ppermute | solution.py:23
  42.1 0.8 %join.1 = bf16[1024,128]{1,0:T(8,128)(2,1)} custom-call(bf16[256,128]{1,0:T(8,128)(2,1)S(1)} %get-tuple-element.25.refs_0_, bf16[256,128]{1,0:T(8,128)(2,1)S(1)} %collective-permute-done.6.refs_1_, bf16[256,128]{1,0:T(8,128)(2,1)S(1)} %collective-permute-done.7.refs_2_, bf16[256,128]{1,0:T(8,128)(2,1)S(1)} %collective-permute-done.8.refs_3_, ...), custom_call_target="tpu_custom_call" | custom-call | tf_op jit(solution)/shard_map/join/pallas_call | solution.py:238
  (15 shorter events, 0.0 us)
Async XLA Ops:
  2.2 8.8 %copy-start.2 = (s32[1,1,8,2]{2,3,1,0:T(2,128)S(1)}, s32[1,1,8,2]{2,3,1,0:T(2,128)}, u32[]{:S(2)}) copy-start(s32[1,1,8,2]{2,3,1,0:T(2,128)} %param.12) | copy-start | bytes 196
  2.2 13.4 %copy-start.1 = (s32[1,1,1024]{2,1,0:T(1,128)S(1)}, s32[1,1,1024]{2,1,0:T(1,128)}, u32[]{:S(2)}) copy-start(s32[1,1,1024]{2,1,0:T(1,128)} %param.15) | copy-start | bytes 12292
  2.3 16.3 %copy-start = (bf16[1,1,2,128,128]{4,3,2,1,0:T(8,128)(2,1)S(1)}, bf16[1,1,2,128,128]{4,3,2,1,0:T(8,128)(2,1)}, u32[]{:S(2)}) copy-start(bf16[1,1,2,128,128]{4,3,2,1,0:T(8,128)(2,1)} %param.14) | copy-start | bytes 196612
  5.1 17.6 %collective-permute-start.4 = (bf16[512,128]{1,0:T(8,128)(2,1)S(1)}, bf16[512,128]{1,0:T(8,128)(2,1)S(1)}, u32[]{:S(2)}, u32[]{:S(2)}) collective-permute-start(bf16[512,128]{1,0:T(8,128)(2,1)S(1)} %get-tuple-element.23), channel_id=1, source_target_pairs={{0,2},{1,3},{2,0},{3,1},{4,6},{5,7},{6,4},{7,5},{8,10},{9,11},{10,... | collective-permute-start | bytes 393224 | tf_op jit(solution)/shard_map/ppermute | solution.py:23
  8.2 14.5 %collective-permute-start.5 = (bf16[512,128]{1,0:T(8,128)(2,1)S(1)}, bf16[512,128]{1,0:T(8,128)(2,1)S(1)}, u32[]{:S(2)}, u32[]{:S(2)}) collective-permute-start(bf16[512,128]{1,0:T(8,128)(2,1)S(1)} %get-tuple-element.24), channel_id=1, source_target_pairs={{0,3},{1,2},{2,1},{3,0},{4,7},{5,6},{6,5},{7,4},{8,11},{9,10},{10,... | collective-permute-start | bytes 393224 | tf_op jit(solution)/shard_map/ppermute | solution.py:23
  9.6 13.1 %collective-permute-start.3 = (bf16[512,128]{1,0:T(8,128)(2,1)S(1)}, bf16[512,128]{1,0:T(8,128)(2,1)S(1)}, u32[]{:S(2)}, u32[]{:S(2)}) collective-permute-start(bf16[512,128]{1,0:T(8,128)(2,1)S(1)} %get-tuple-element.22), channel_id=1, source_target_pairs={{0,1},{1,0},{2,3},{3,2},{4,5},{5,4},{6,7},{7,6},{8,9},{9,8},{10,11... | collective-permute-start | bytes 393224 | tf_op jit(solution)/shard_map/ppermute | solution.py:23
  9.8 12.9 %collective-permute-start.2 = (bf16[256,128]{1,0:T(8,128)(2,1)S(1)}, bf16[256,128]{1,0:T(8,128)(2,1)S(1)}, u32[]{:S(2)}, u32[]{:S(2)}) collective-permute-start(bf16[256,128]{1,0:T(8,128)(2,1)S(1)} %get-tuple-element.20), channel_id=1, source_target_pairs={{0,8},{8,16},{16,24},{1,9},{9,17},{17,25},{2,10},{10,18},{18,26},{... | collective-permute-start | bytes 196616 | tf_op jit(solution)/shard_map/ppermute | solution.py:273
  11.1 4.6 %collective-permute-start = (s32[2,8]{1,0:T(2,128)S(1)}, s32[2,8]{1,0:T(2,128)S(1)}, u32[]{:S(2)}, u32[]{:S(2)}) collective-permute-start(s32[2,8]{1,0:T(2,128)S(1)} %bitcast.12), channel_id=1, source_target_pairs={{0,4},{1,5},{2,6},{3,7},{4,0},{5,1},{6,2},{7,3},{8,12},{9,13},{10,... | collective-permute-start | bytes 200 | tf_op jit(solution)/shard_map/ppermute | solution.py:23
  15.7 5.5 %collective-permute-start.1 = (s32[8,128]{1,0:T(8,128)S(1)}, s32[8,128]{1,0:T(8,128)S(1)}, u32[]{:S(2)}, u32[]{:S(2)}) collective-permute-start(s32[8,128]{1,0:T(8,128)S(1)} %bitcast.10), channel_id=1, source_target_pairs={{0,4},{1,5},{2,6},{3,7},{4,0},{5,1},{6,2},{7,3},{8,12},{9,13},{10,... | collective-permute-start | bytes 12296 | tf_op jit(solution)/shard_map/ppermute | solution.py:23
  23.6 9.6 %collective-permute-start.10 = (bf16[256,128]{1,0:T(8,128)(2,1)S(1)}, bf16[256,128]{1,0:T(8,128)(2,1)S(1)}, u32[]{:S(2)}, u32[]{:S(2)}) collective-permute-start(bf16[256,128]{1,0:T(8,128)(2,1)S(1)} %get-tuple-element.30), channel_id=1, source_target_pairs={{0,5},{1,4},{2,7},{3,6},{4,1},{5,0},{6,3},{7,2},{8,13},{9,12},{10,... | collective-permute-start | bytes 196616 | tf_op jit(solution)/shard_map/ppermute | solution.py:23
  26.5 8.7 %collective-permute-start.11 = (bf16[256,128]{1,0:T(8,128)(2,1)S(1)}, bf16[256,128]{1,0:T(8,128)(2,1)S(1)}, u32[]{:S(2)}, u32[]{:S(2)}) collective-permute-start(bf16[256,128]{1,0:T(8,128)(2,1)S(1)} %get-tuple-element.31), channel_id=1, source_target_pairs={{0,6},{1,7},{2,4},{3,5},{4,2},{5,3},{6,0},{7,1},{8,14},{9,15},{10,... | collective-permute-start | bytes 196616 | tf_op jit(solution)/shard_map/ppermute | solution.py:23
  28.5 10.5 %collective-permute-start.12 = (bf16[256,128]{1,0:T(8,128)(2,1)S(1)}, bf16[256,128]{1,0:T(8,128)(2,1)S(1)}, u32[]{:S(2)}, u32[]{:S(2)}) collective-permute-start(bf16[256,128]{1,0:T(8,128)(2,1)S(1)} %get-tuple-element.32), channel_id=1, source_target_pairs={{0,7},{1,6},{2,5},{3,4},{4,3},{5,2},{6,1},{7,0},{8,15},{9,14},{10,... | collective-permute-start | bytes 196616 | tf_op jit(solution)/shard_map/ppermute | solution.py:23
  30.3 9.9 %collective-permute-start.9 = (bf16[256,128]{1,0:T(8,128)(2,1)S(1)}, bf16[256,128]{1,0:T(8,128)(2,1)S(1)}, u32[]{:S(2)}, u32[]{:S(2)}) collective-permute-start(bf16[256,128]{1,0:T(8,128)(2,1)S(1)} %get-tuple-element.29), channel_id=1, source_target_pairs={{0,4},{1,5},{2,6},{3,7},{4,0},{5,1},{6,2},{7,3},{8,12},{9,13},{10,... | collective-permute-start | bytes 196616 | tf_op jit(solution)/shard_map/ppermute | solution.py:23
  31.1 9.1 %collective-permute-start.6 = (bf16[256,128]{1,0:T(8,128)(2,1)S(1)}, bf16[256,128]{1,0:T(8,128)(2,1)S(1)}, u32[]{:S(2)}, u32[]{:S(2)}) collective-permute-start(bf16[256,128]{1,0:T(8,128)(2,1)S(1)} %get-tuple-element.26), channel_id=1, source_target_pairs={{0,1},{1,0},{2,3},{3,2},{4,5},{5,4},{6,7},{7,6},{8,9},{9,8},{10,11... | collective-permute-start | bytes 196616 | tf_op jit(solution)/shard_map/ppermute | solution.py:23
  33.2 7.1 %collective-permute-start.7 = (bf16[256,128]{1,0:T(8,128)(2,1)S(1)}, bf16[256,128]{1,0:T(8,128)(2,1)S(1)}, u32[]{:S(2)}, u32[]{:S(2)}) collective-permute-start(bf16[256,128]{1,0:T(8,128)(2,1)S(1)} %get-tuple-element.27), channel_id=1, source_target_pairs={{0,2},{1,3},{2,0},{3,1},{4,6},{5,7},{6,4},{7,5},{8,10},{9,11},{10,... | collective-permute-start | bytes 196616 | tf_op jit(solution)/shard_map/ppermute | solution.py:23
  35.3 6.8 %collective-permute-start.8 = (bf16[256,128]{1,0:T(8,128)(2,1)S(1)}, bf16[256,128]{1,0:T(8,128)(2,1)S(1)}, u32[]{:S(2)}, u32[]{:S(2)}) collective-permute-start(bf16[256,128]{1,0:T(8,128)(2,1)S(1)} %get-tuple-element.28), channel_id=1, source_target_pairs={{0,3},{1,2},{2,1},{3,0},{4,7},{5,6},{6,5},{7,4},{8,11},{9,10},{10,... | collective-permute-start | bytes 196616 | tf_op jit(solution)/shard_map/ppermute | solution.py:23
where the time goes:
time: 43 us; the launch traced here: 42.8 us
  starting transfers between devices  26 us (60%)
  Pallas kernels  11.6 us (27%)
  waiting for transfers between devices  5.11 us (12%)
    ppermute x12, starting transfers between devices, swap(): lax.ppermute(value, 'dom', [(source, source ^ step) for source in range(c...  24.7 us
    ppermute x12, waiting for transfers between devices, swap(): lax.ppermute(value, 'dom', [(source, source ^ step) for source in range(c...  5.11 us
    pallas_call x2, Pallas kernels, form_parts(): pl.pallas_call(functools.partial(parts_kernel, steps, load), out_shape=sh...  5.06 us
    pallas_call x2, Pallas kernels, choose(): pl.pallas_call(functools.partial(choose_kernel, steps, bool(extra)), out_...  4.1 us
    pallas_call x2, Pallas kernels, place(): pl.pallas_call(functools.partial(place_kernel, steps, far, share), out_sh...  1.65 us
    ppermute x1, starting transfers between devices, on_device(): lax.ppermute(rim, 'slab', [(source, source + 1) for source in range(slabs...  1.28 us
  transfers between devices with their start and end apart: 13, of which 4 were waited for; matrix products, arithmetic and copies ran while one was open for 0% of the time, Pallas kernels for 12%

commit v1 on v0

--- a/solution.py
+++ b/solution.py
@@ -23,28 +23,52 @@
     return lax.ppermute(value, "dom", [(source, source ^ step) for source in range(count)])
 
 
-def parts_kernel(steps, load, *refs):
-    block_hbm, count_hbm, target_hbm, donors, weights = refs[:5]
-    outs = refs[5 : 5 + len(steps)]
-    extra = refs[5 + len(steps)]
-    held_d = extra if load else donors
-    block_of, count_of, target_of, held_w, sems, sem_w = refs[-6:]
-    rows = held_w.shape[2]
-    capacity = held_w.shape[1]
-    width = held_d.shape[1]
-    half = block_of.shape[0] // 2
-    places = outs[0].shape[0] // (2 * rows)
+def form_part(out, side, p, block_of, count_of, target_of, weight, block):
+    capacity = block_of.shape[1]
+    rows, width = weight(0).shape[0], out.shape[1]
+    places = out.shape[0] // (2 * rows)
+    total = None
+    for c in range(0, capacity, 2):
+        left = jnp.concatenate([weight(c), weight(c + 1)], axis=1)
+        pieces = []
+        for k in (c, c + 1):
+            value = block(k)
+            live = k < count_of[p]
+            kept = []
+            for t in range(places):
+                wanted = jnp.logical_and(live, target_of[p, k] == t)
+                kept.append(jnp.where(wanted, value, jnp.zeros_like(value)))
+            pieces.append(jnp.concatenate(kept, axis=1))
+        right = jnp.concatenate(pieces, axis=0)
+        prod = jnp.dot(left, right, preferred_element_type=jnp.float32)
+        total = prod if total is None else total + prod
+    for t in range(places):
+        at = (side * places + t) * rows
+        out[at : at + rows] = total[:, t * width : (t + 1) * width].astype(out.dtype)
+
+
+def owners_of(steps, half):
     me = lax.axis_index("dom")
-    owners = []
+    found = []
     for step in steps:
-        owners += [jnp.bitwise_xor(me, step), jnp.bitwise_xor(me, step + half)]
+        found += [jnp.bitwise_xor(me, step), jnp.bitwise_xor(me, step + half)]
+    return found
+
+
+def gather_kernel(steps, block_hbm, count_hbm, target_hbm, donors, weights, *refs):
+    outs = refs[: len(steps)]
+    rim = refs[len(steps)]
+    block_of, count_of, target_of, held_w, held_d, sems, sem_w, sem_d = refs[len(steps) + 1 :]
+    capacity, rows = held_w.shape[1:3]
+    owners = owners_of(steps, block_of.shape[0] // 2)
     tables = [
         pltpu.make_async_copy(block_hbm, block_of, sems.at[0]),
         pltpu.make_async_copy(count_hbm, count_of, sems.at[1]),
         pltpu.make_async_copy(target_hbm, target_of, sems.at[2]),
     ]
-    if load:
-        tables.append(pltpu.make_async_copy(donors, held_d, sems.at[3]))
+    tail = pltpu.make_async_copy(
+        donors.at[pl.ds(donors.shape[0] - rim.shape[0], rim.shape[0])], rim, sems.at[3]
+    )
     loads = [
         pltpu.make_async_copy(weights.at[p], held_w.at[i], sem_w.at[i])
         for i, p in enumerate(owners)
@@ -54,60 +78,91 @@
     for copy in tables:
         copy.wait()
     for i, p in enumerate(owners):
-        loads[i].wait()
-        total = None
-        for c in range(0, capacity, 2):
-            left = jnp.concatenate([held_w[i, c], held_w[i, c + 1]], axis=1)
-            pieces = []
-            for k in (c, c + 1):
-                row = pl.multiple_of(block_of[p, k] * rows, rows)
-                block = held_d[pl.ds(row, rows)]
-                live = k < count_of[p]
-                kept = []
-                for t in range(places):
-                    wanted = jnp.logical_and(live, target_of[p, k] == t)
-                    kept.append(jnp.where(wanted, block, jnp.zeros_like(block)))
-                pieces.append(jnp.concatenate(kept, axis=1))
-            right = jnp.concatenate(pieces, axis=0)
-            prod = jnp.dot(left, right, preferred_element_type=jnp.float32)
-            total = prod if total is None else total + prod
-        for t in range(places):
-            at = ((i % 2) * places + t) * rows
-            outs[i // 2][at : at + rows] = total[:, t * width : (t + 1) * width].astype(
-                outs[0].dtype
+        for c in range(capacity):
+            row = pl.multiple_of(block_of[p, c] * rows, rows)
+            copy = pltpu.make_async_copy(
+                donors.at[pl.ds(row, rows)], held_d.at[i, c], sem_d.at[i, c]
             )
-    if not load:
-        extra[...] = held_d[held_d.shape[0] - extra.shape[0] : held_d.shape[0]]
-
-
-def form_parts(steps, tables, donors, weights, places, load, extra_rows):
-    _, capacity, rows, _ = weights.shape
+            copy.start()
+            loads.append(copy)
+    tail.start()
+    for copy in loads:
+        copy.wait()
+    for i, p in enumerate(owners):
+        form_part(
+            outs[i // 2], i % 2, p, block_of, count_of, target_of,
+            lambda c, i=i: held_w[i, c], lambda c, i=i: held_d[i, c],
+        )
+    tail.wait()
+
+
+def part_shapes(steps, donors, weights, places):
+    rows = 2 * places * weights.shape[2]
+    return [jax.ShapeDtypeStruct((rows, donors.shape[1]), jnp.bfloat16)] * len(steps)
+
+
+def gather_parts(steps, tables, donors, weights, places, rim_rows):
+    capacity, rows = weights.shape[1:3]
     width = donors.shape[1]
-    shapes = [jax.ShapeDtypeStruct((2 * places * rows, width), jnp.bfloat16)] * len(steps)
-    shapes.append(jax.ShapeDtypeStruct((extra_rows, width), donors.dtype))
+    shapes = part_shapes(steps, donors, weights, places)
+    shapes.append(jax.ShapeDtypeStruct((rim_rows, width), donors.dtype))
     in_hbm = functools.partial(pltpu.with_memory_space_constraint, memory_space=pltpu.HBM)
-    held = jax.ShapeDtypeStruct((2 * len(steps), capacity, rows, rows), weights.dtype)
-    return pl.pallas_call(
-        functools.partial(parts_kernel, steps, load),
+    held_w = jax.ShapeDtypeStruct((2 * len(steps), capacity, rows, rows), weights.dtype)
+    held_d = jax.ShapeDtypeStruct((2 * len(steps), capacity, rows, width), donors.dtype)
+    return pl.pallas_call(
+        functools.partial(gather_kernel, steps),
         out_shape=shapes,
-        in_specs=[HBM, HBM, HBM, HBM if load else VMEM, HBM],
+        in_specs=[HBM] * 5,
         out_specs=[VMEM] * len(shapes),
         scratch_shapes=[pltpu.SMEM(table.shape, table.dtype) for table in tables]
         + [
-            pltpu.VMEM(held.shape, held.dtype),
+            pltpu.VMEM(held_w.shape, held_w.dtype),
+            pltpu.VMEM(held_d.shape, held_d.dtype),
             pltpu.SemaphoreType.DMA((4,)),
             pltpu.SemaphoreType.DMA((2 * len(steps),)),
+            pltpu.SemaphoreType.DMA((2 * len(steps), capacity)),
         ],
         compiler_params=pltpu.CompilerParams(
-            vmem_limit_bytes=nbytes(held, donors, *shapes) + MARGIN
+            vmem_limit_bytes=nbytes(held_w, held_d, *shapes) + MARGIN
         ),
         cost_estimate=pl.CostEstimate(
-            flops=8 * len(steps) * capacity * rows * rows * width,
-            bytes_accessed=nbytes(held, donors),
+            flops=4 * held_w.size * width, bytes_accessed=nbytes(held_w), transcendentals=0
+        ),
+        name="gather",
+    )(*map(in_hbm, [*tables, donors, weights]))
+
+
+def parts_kernel(steps, block_of, count_of, target_of, donors, weights, *outs):
+    rows = weights.shape[2]
+    for i, p in enumerate(owners_of(steps, block_of.shape[0] // 2)):
+
+        def block(c, p=p):
+            row = pl.multiple_of(block_of[p, c] * rows, rows)
+            return donors[pl.ds(row, rows)]
+
+        form_part(
+            outs[i // 2], i % 2, p, block_of, count_of, target_of,
+            lambda c, p=p: weights[p, c], block,
+        )
+
+
+def form_parts(steps, tables, donors, weights, places):
+    shapes = part_shapes(steps, donors, weights, places)
+    return pl.pallas_call(
+        functools.partial(parts_kernel, steps),
+        out_shape=shapes,
+        in_specs=[SMEM] * 3 + [VMEM] * 2,
+        out_specs=[VMEM] * len(shapes),
+        compiler_params=pltpu.CompilerParams(
+            vmem_limit_bytes=nbytes(weights, donors, *shapes) + MARGIN
+        ),
+        cost_estimate=pl.CostEstimate(
+            flops=4 * donors.size * len(steps),
+            bytes_accessed=nbytes(weights),
             transcendentals=0,
         ),
         name="parts",
-    )(*map(in_hbm, tables), in_hbm(donors) if load else donors, in_hbm(weights))
+    )(*tables, donors, weights)
 
 
 def choose_kernel(steps, with_halo, place_of, order, *refs):
@@ -123,22 +178,22 @@
         starts += [place_of[t, q] * rows for t in range(places)]
 
     def fill(j, carry):
-        wanted = jnp.broadcast_to(order[pl.ds(j, 1), :], (rows, rows)).T - lane
+        wanted = (jnp.broadcast_to(order[pl.ds(j, 1), :], (rows, rows)).T - lane).astype(jnp.int16)
         row = pl.multiple_of(j * rows, rows)
         for b, begin in enumerate(starts):
             chosen[pl.ds(row, rows), b * rows : (b + 1) * rows] = jnp.where(
-                wanted == begin, 1.0, 0.0
+                wanted == begin.astype(jnp.int16), jnp.bfloat16(1), jnp.bfloat16(0)
+            )
+        if with_halo:
+            first = jnp.where(wanted == 0, jnp.bfloat16(1), jnp.bfloat16(0))
+            both = jnp.concatenate([halo_w[h] for h in range(halo_w.shape[0])], axis=1)
+            chosen[pl.ds(row, rows), len(starts) * rows :] = jnp.dot(
+                first, both, preferred_element_type=jnp.float32
             ).astype(jnp.bfloat16)
-        if with_halo:
-            first = jnp.where(wanted == 0, 1.0, 0.0).astype(jnp.bfloat16)
-            for h in range(halo_w.shape[0]):
-                at = (len(starts) + h) * rows
-                chosen[pl.ds(row, rows), at : at + rows] = jnp.dot(
-                    first, halo_w[h], preferred_element_type=jnp.float32
-                ).astype(jnp.bfloat16)
         return carry
 
-    lax.fori_loop(0, order.shape[0], fill, 0)
+    for j in range(order.shape[0]):
+        fill(j, 0)
 
 
 def choose(steps, place_of, order, halo_w=None):
@@ -172,20 +227,14 @@
     begin = pl.multiple_of(begin, lot)
     depth = parts[0].shape[0] // 2
     for side, matrix in enumerate((own, other)):
-        total = None
-        for i, part in enumerate(parts):
-            prod = jnp.dot(
-                matrix[pl.ds(begin, lot), i * depth : (i + 1) * depth],
-                part[side * depth : (side + 1) * depth],
-                preferred_element_type=jnp.float32,
-            )
-            total = prod if total is None else total + prod
+        stack = [part[side * depth : (side + 1) * depth] for part in parts]
         if side == 0:
-            total += jnp.dot(
-                matrix[pl.ds(begin, lot), len(parts) * depth :],
-                rim[...],
-                preferred_element_type=jnp.float32,
-            )
+            stack.append(rim[...])
+        total = jnp.dot(
+            matrix[pl.ds(begin, lot)],
+            jnp.concatenate(stack, axis=0),
+            preferred_element_type=jnp.float32,
+        )
         rows_of[side] = total
     for step, out in zip(steps, outs):
         at = pl.multiple_of(lax.rem(jnp.bitwise_xor(me, step), half) * share, share)
@@ -249,6 +298,11 @@
     )(*chunks)
 
 
+def near_steps(count):
+    half = count // 2
+    return [half - 1] + list(range(1, half - 1))
+
+
 def on_device(
     donors, send_block, send_count, send_target, target_block, weights, halo_weights, permute
 ):
@@ -260,12 +314,11 @@
     share = permute.shape[-1] // count
     tables = send_block[0, 0], send_count[0, 0], send_target[0, 0]
     places = target_block.shape[-1]
-    form = functools.partial(form_parts, tables=tables, weights=weights[0, 0], places=places)
-    near = list(range(1, half))
-    *first, held = form(near[:1], donors=donors, load=True, extra_rows=donors.shape[0])
-    *second, rim = form(near[1:] + [0], donors=held, load=False, extra_rows=rim_rows)
-    own_part = second.pop()
-    arrived = [swap(part, step) for part, step in zip(first + second, near)]
+    near = near_steps(count)
+    *first, rim = gather_parts(near[:1], tables, donors, weights[0, 0], places, rim_rows)
+    second = form_parts(near[1:], tables, donors, weights[0, 0], places)
+    third = form_parts([0], tables, donors, weights[0, 0], places)
+    arrived = [swap(part, step) for part, step in zip([*first, *second], near)]
     order = permute[0, 0].reshape(-1, block_rows)
     other_order = swap(order, half)
     table = target_block[0, 0].T
@@ -273,7 +326,7 @@
     rim = lax.ppermute(rim, "slab", [(source, source + 1) for source in range(slabs - 1)])
     own = choose([0] + near, table, order, halo_weights[0, 0])
     other = choose([0] + near, other_table, other_order)
-    parts = [own_part] + arrived
+    parts = [*third, *arrived]
     far_steps = list(range(count - 1, half - 1, -1))
     far = place(far_steps, True, share, own, other, rim, parts)
     close_steps = list(range(half - 1, -1, -1))

time: 43 us -> 46.1 us (1.072)
  local copies, waits for them, and re-layouts: 0.02 us -> 5.25 us
  Pallas kernels: 11.6 us -> 9.02 us
    unnamed x6 -> x26, local copies, waits for them, and re-layouts: 0.02 us -> 5.25 us
    pallas_call x2, Pallas kernels: 4.1 us -> 2.01 us  [choose(): pl.pallas_call(functools.partial(choose_kernel, steps, bool(extra)), out_...]
    pallas_call x2 -> x3, Pallas kernels: 5.06 us -> 4.59 us  [the longest x1 2.44 us: gather_parts(): pl.pallas_call(functools.partial(gather_kernel, steps), out_shape=shapes,...]
  transfers between devices with their start and end apart: 13 -> 13, of which waited for: 4 -> 4; matrix products, arithmetic and copies ran while one was open for 0% -> 0% of each run, Pallas kernels for 12% -> 14%
where the time goes in v1:
time: 46.1 us; the launch traced here: 45.8 us
  starting transfers between devices  26.3 us (57%)
  Pallas kernels  9.02 us (20%)
  local copies, waits for them, and re-layouts  5.25 us (11%)
  waiting for transfers between devices  4.97 us (11%)
    ppermute x12, starting transfers between devices, swap(): lax.ppermute(value, 'dom', [(source, source ^ step) for source in range(c...  24.9 us
    unnamed x26, local copies, waits for them, and re-layouts  5.25 us
    ppermute x12, waiting for transfers between devices, swap(): lax.ppermute(value, 'dom', [(source, source ^ step) for source in range(c...  4.97 us
    pallas_call x1, Pallas kernels, gather_parts(): pl.pallas_call(functools.partial(gather_kernel, steps), out_shape=shapes,...  2.44 us
    pallas_call x2, Pallas kernels, form_parts(): pl.pallas_call(functools.partial(parts_kernel, steps), out_shape=shapes,...  2.14 us
    pallas_call x2, Pallas kernels, choose(): pl.pallas_call(functools.partial(choose_kernel, steps, bool(extra)), out_...  2.01 us
    pallas_call x2, Pallas kernels, place(): pl.pallas_call(functools.partial(place_kernel, steps, far, share), out_sh...  1.65 us
    ppermute x1, starting transfers between devices, on_device(): lax.ppermute(rim, 'slab', [(source, source + 1) for source in range(slabs...  1.42 us
  transfers between devices with their start and end apart: 13, of which 4 were waited for; matrix products, arithmetic and copies ran while one was open for 0% of the time, Pallas kernels for 14%

profile of v1, /device:TPU:0, one launch (start us, length us, event | category | flops | bytes accessed | tf_op | source)
XLA Modules:
  0.0 45.8 jit_solution(11466757642095077909)
XLA Ops:
  0.0 1.6 %copy-done = bf16[8192,128]{1,0:T(8,128)(2,1)S(1)} copy-done((bf16[8192,128]{1,0:T(8,128)(2,1)S(1)}, bf16[8192,128]{1,0:T(8,128)(2,1)}, u32[]{:S(2)}) %copy-start) | copy-done | bytes 2097176
  1.6 1.6 %copy-done.2 = bf16[1,1,8,8,128,128]{5,4,3,2,1,0:T(8,128)(2,1)S(1)} copy-done((bf16[1,1,8,8,128,128]{5,4,3,2,1,0:T(8,128)(2,1)S(1)}, bf16[1,1,8,8,128,128]{5,4,3,2,1,0:T(8,128)(2,1)}, u32[]{:S(2)}) %copy-start.2) | copy-done | bytes 2097176
  5.2 1.1 %parts.3 = (bf16[512,128]{1,0:T(8,128)(2,1)S(1)}, bf16[512,128]{1,0:T(8,128)(2,1)S(1)}) custom-call(s32[8,8]{1,0:T(8,128)S(1)} %bitcast.14, s32[8]{0:T(128)S(1)} %bitcast.20, s32[8,8]{1,0:T(8,128)S(1)} %bitcast.17, bf16[8192,128]{1,0:T(8,128)(2,1)S(1)} %copy-done, bf16[8,8,128,128]{3,2,1,0:T(8,128)(2,1)S(1)} %bitcast.10), custom_call_target="tpu_custom_call" | custom-call | flops 8388608 | bytes 2097152 | tf_op jit(solution)/shard_map/parts/pallas_call | solution.py:151
  6.4 3.1 %collective-permute-start.4 = (bf16[512,128]{1,0:T(8,128)(2,1)S(1)}, bf16[512,128]{1,0:T(8,128)(2,1)S(1)}, u32[]{:S(2)}, u32[]{:S(2)}) collective-permute-start(bf16[512,128]{1,0:T(8,128)(2,1)S(1)} %get-tuple-element.19), channel_id=1, source_target_pairs={{0,1},{1,0},{2,3},{3,2},{4,5},{5,4},{6,7},{7,6},{8,9},{9,8},{10,11... | collective-permute-start | bytes 393224 | tf_op jit(solution)/shard_map/ppermute | solution.py:23
  9.4 1.6 %collective-permute-start.5 = (bf16[512,128]{1,0:T(8,128)(2,1)S(1)}, bf16[512,128]{1,0:T(8,128)(2,1)S(1)}, u32[]{:S(2)}, u32[]{:S(2)}) collective-permute-start(bf16[512,128]{1,0:T(8,128)(2,1)S(1)} %get-tuple-element.20), channel_id=1, source_target_pairs={{0,2},{1,3},{2,0},{3,1},{4,6},{5,7},{6,4},{7,5},{8,10},{9,11},{10,... | collective-permute-start | bytes 393224 | tf_op jit(solution)/shard_map/ppermute | solution.py:23
  11.0 2.4 %gather.1 = (bf16[512,128]{1,0:T(8,128)(2,1)S(1)}, bf16[256,128]{1,0:T(8,128)(2,1)S(1)}) custom-call(s32[8,8]{1,0:T(8,128)} %bitcast.13, s32[8]{0:T(128)} %bitcast.19, s32[8,8]{1,0:T(8,128)} %bitcast.16, bf16[8192,128]{1,0:T(8,128)(2,1)} %donors.5, bf16[8,8,128,128]{3,2,1,0:T(8,128)(2,1)} %bitcast.9), custom_call_target="tpu_custom_call" | custom-call | flops 134217728 | bytes 524288 | tf_op jit(solution)/shard_map/gather/pallas_call | solution.py:112
  13.6 1.4 %collective-permute-start.2 = (bf16[256,128]{1,0:T(8,128)(2,1)S(1)}, bf16[256,128]{1,0:T(8,128)(2,1)S(1)}, u32[]{:S(2)}, u32[]{:S(2)}) collective-permute-start(bf16[256,128]{1,0:T(8,128)(2,1)S(1)} %get-tuple-element.17), channel_id=1, source_target_pairs={{0,8},{8,16},{16,24},{1,9},{9,17},{17,25},{2,10},{10,18},{18,26},{... | collective-permute-start | bytes 196616 | tf_op jit(solution)/shard_map/ppermute | solution.py:326
  15.0 3.0 %collective-permute-start = (s32[2,8]{1,0:T(2,128)S(1)}, s32[2,8]{1,0:T(2,128)S(1)}, u32[]{:S(2)}, u32[]{:S(2)}) collective-permute-start(s32[2,8]{1,0:T(2,128)S(1)} %bitcast.24), channel_id=1, source_target_pairs={{0,4},{1,5},{2,6},{3,7},{4,0},{5,1},{6,2},{7,3},{8,12},{9,13},{10,... | collective-permute-start | bytes 200 | tf_op jit(solution)/shard_map/ppermute | solution.py:23
  18.1 1.6 %collective-permute-done.place_of = s32[2,8]{1,0:T(2,128)S(1)} collective-permute-done((s32[2,8]{1,0:T(2,128)S(1)}, s32[2,8]{1,0:T(2,128)S(1)}, u32[]{:S(2)}, u32[]{:S(2)}) %collective-permute-start) | collective-permute-done | bytes 96 | tf_op jit(solution)/shard_map/ppermute | solution.py:23
  19.6 2.9 %collective-permute-start.1 = (s32[8,128]{1,0:T(8,128)S(1)}, s32[8,128]{1,0:T(8,128)S(1)}, u32[]{:S(2)}, u32[]{:S(2)}) collective-permute-start(s32[8,128]{1,0:T(8,128)S(1)} %bitcast.22), channel_id=1, source_target_pairs={{0,4},{1,5},{2,6},{3,7},{4,0},{5,1},{6,2},{7,3},{8,12},{9,13},{10,... | collective-permute-start | bytes 12296 | tf_op jit(solution)/shard_map/ppermute | solution.py:23
  22.5 1.1 %choose.2.own = bf16[1024,1280]{1,0:T(8,128)(2,1)S(1)} custom-call(s32[2,8]{1,0:T(2,128)S(1)} %bitcast.25, s32[8,128]{1,0:T(8,128)S(1)} %bitcast.23, bf16[2,128,128]{2,1,0:T(8,128)(2,1)S(1)} %bitcast.12), custom_call_target="tpu_custom_call" | custom-call | flops 1310720 | bytes 2621440 | tf_op jit(solution)/shard_map/choose/pallas_call | solution.py:204
  23.7 1.0 %parts.2.refs_0_ = bf16[512,128]{1,0:T(8,128)(2,1)S(1)} custom-call(s32[8,8]{1,0:T(8,128)S(1)} %bitcast.15, s32[8]{0:T(128)S(1)} %bitcast.21, s32[8,8]{1,0:T(8,128)S(1)} %bitcast.18, bf16[8192,128]{1,0:T(8,128)(2,1)S(1)} %copy-done.1, bf16[8,8,128,128]{3,2,1,0:T(8,128)(2,1)S(1)} %bitcast.11), custom_call_target="tpu_custom_call" | custom-call | flops 4194304 | bytes 2097152 | tf_op jit(solution)/shard_map/parts/pallas_call | solution.py:151
  24.7 0.9 %choose.3.other = bf16[1024,1024]{1,0:T(8,128)(2,1)S(1)} custom-call(s32[2,8]{1,0:T(2,128)S(1)} %collective-permute-done.place_of, s32[8,128]{1,0:T(8,128)S(1)} %collective-permute-done.1.order), custom_call_target="tpu_custom_call" | custom-call | flops 1048576 | bytes 2097152 | tf_op jit(solution)/shard_map/choose/pallas_call | solution.py:204
  25.7 0.8 %place.3 = (bf16[256,128]{1,0:T(8,128)(2,1)S(1)}, bf16[256,128]{1,0:T(8,128)(2,1)S(1)}, bf16[256,128]{1,0:T(8,128)(2,1)S(1)}, bf16[256,128]{1,0:T(8,128)(2,1)S(1)}) custom-call(bf16[1024,1280]{1,0:T(8,128)(2,1)S(1)} %choose.2.own, bf16[1024,1024]{1,0:T(8,128)(2,1)S(1)} %choose.3.other, bf16[256,128]{1,0:T(8,128)(2,1)S(1)} %collective-permute-done.2.rim, ...), custom_call_target="tpu_custom_call" | custom-call | flops 335544320 | bytes 2621440 | tf_op jit(solution)/shard_map/place/pallas_call | solution.py:251
  26.5 3.2 %collective-permute-start.10 = (bf16[256,128]{1,0:T(8,128)(2,1)S(1)}, bf16[256,128]{1,0:T(8,128)(2,1)S(1)}, u32[]{:S(2)}, u32[]{:S(2)}) collective-permute-start(bf16[256,128]{1,0:T(8,128)(2,1)S(1)} %get-tuple-element.26), channel_id=1, source_target_pairs={{0,5},{1,4},{2,7},{3,6},{4,1},{5,0},{6,3},{7,2},{8,13},{9,12},{10,... | collective-permute-start | bytes 196616 | tf_op jit(solution)/shard_map/ppermute | solution.py:23
  29.7 1.6 %collective-permute-start.11 = (bf16[256,128]{1,0:T(8,128)(2,1)S(1)}, bf16[256,128]{1,0:T(8,128)(2,1)S(1)}, u32[]{:S(2)}, u32[]{:S(2)}) collective-permute-start(bf16[256,128]{1,0:T(8,128)(2,1)S(1)} %get-tuple-element.27), channel_id=1, source_target_pairs={{0,6},{1,7},{2,4},{3,5},{4,2},{5,3},{6,0},{7,1},{8,14},{9,15},{10,... | collective-permute-start | bytes 196616 | tf_op jit(solution)/shard_map/ppermute | solution.py:23
  31.3 2.3 %collective-permute-start.12 = (bf16[256,128]{1,0:T(8,128)(2,1)S(1)}, bf16[256,128]{1,0:T(8,128)(2,1)S(1)}, u32[]{:S(2)}, u32[]{:S(2)}) collective-permute-start(bf16[256,128]{1,0:T(8,128)(2,1)S(1)} %get-tuple-element.28), channel_id=1, source_target_pairs={{0,7},{1,6},{2,5},{3,4},{4,3},{5,2},{6,1},{7,0},{8,15},{9,14},{10,... | collective-permute-start | bytes 196616 | tf_op jit(solution)/shard_map/ppermute | solution.py:23
  33.6 0.8 %place.2 = (bf16[256,128]{1,0:T(8,128)(2,1)S(1)}, bf16[256,128]{1,0:T(8,128)(2,1)S(1)}, bf16[256,128]{1,0:T(8,128)(2,1)S(1)}, bf16[256,128]{1,0:T(8,128)(2,1)S(1)}) custom-call(bf16[1024,1280]{1,0:T(8,128)(2,1)S(1)} %choose.2.own, bf16[1024,1024]{1,0:T(8,128)(2,1)S(1)} %choose.3.other, bf16[256,128]{1,0:T(8,128)(2,1)S(1)} %collective-permute-done.2.rim, ...), custom_call_target="tpu_custom_call" | custom-call | flops 335544320 | bytes 2621440 | tf_op jit(solution)/shard_map/place/pallas_call | solution.py:251
  34.5 1.5 %collective-permute-start.6 = (bf16[256,128]{1,0:T(8,128)(2,1)S(1)}, bf16[256,128]{1,0:T(8,128)(2,1)S(1)}, u32[]{:S(2)}, u32[]{:S(2)}) collective-permute-start(bf16[256,128]{1,0:T(8,128)(2,1)S(1)} %get-tuple-element.22), channel_id=1, source_target_pairs={{0,1},{1,0},{2,3},{3,2},{4,5},{5,4},{6,7},{7,6},{8,9},{9,8},{10,11... | collective-permute-start | bytes 196616 | tf_op jit(solution)/shard_map/ppermute | solution.py:23
  36.1 2.5 %collective-permute-start.7 = (bf16[256,128]{1,0:T(8,128)(2,1)S(1)}, bf16[256,128]{1,0:T(8,128)(2,1)S(1)}, u32[]{:S(2)}, u32[]{:S(2)}) collective-permute-start(bf16[256,128]{1,0:T(8,128)(2,1)S(1)} %get-tuple-element.23), channel_id=1, source_target_pairs={{0,2},{1,3},{2,0},{3,1},{4,6},{5,7},{6,4},{7,5},{8,10},{9,11},{10,... | collective-permute-start | bytes 196616 | tf_op jit(solution)/shard_map/ppermute | solution.py:23
  38.6 3.2 %collective-permute-start.8 = (bf16[256,128]{1,0:T(8,128)(2,1)S(1)}, bf16[256,128]{1,0:T(8,128)(2,1)S(1)}, u32[]{:S(2)}, u32[]{:S(2)}) collective-permute-start(bf16[256,128]{1,0:T(8,128)(2,1)S(1)} %get-tuple-element.24), channel_id=1, source_target_pairs={{0,3},{1,2},{2,1},{3,0},{4,7},{5,6},{6,5},{7,4},{8,11},{9,10},{10,... | collective-permute-start | bytes 196616 | tf_op jit(solution)/shard_map/ppermute | solution.py:23
  41.8 1.3 %collective-permute-done.9.refs_4_ = bf16[256,128]{1,0:T(8,128)(2,1)S(1)} collective-permute-done((bf16[256,128]{1,0:T(8,128)(2,1)S(1)}, bf16[256,128]{1,0:T(8,128)(2,1)S(1)}, u32[]{:S(2)}, u32[]{:S(2)}) %collective-permute-start.9) | collective-permute-done | bytes 65568 | tf_op jit(solution)/shard_map/ppermute | solution.py:23
  43.1 1.9 %collective-permute-done.8.refs_3_ = bf16[256,128]{1,0:T(8,128)(2,1)S(1)} collective-permute-done((bf16[256,128]{1,0:T(8,128)(2,1)S(1)}, bf16[256,128]{1,0:T(8,128)(2,1)S(1)}, u32[]{:S(2)}, u32[]{:S(2)}) %collective-permute-start.8) | collective-permute-done | bytes 65568 | tf_op jit(solution)/shard_map/ppermute | solution.py:23
  45.0 0.8 %join.1 = bf16[1024,128]{1,0:T(8,128)(2,1)} custom-call(bf16[256,128]{1,0:T(8,128)(2,1)S(1)} %get-tuple-element.21.refs_0_, bf16[256,128]{1,0:T(8,128)(2,1)S(1)} %collective-permute-done.6.refs_1_, bf16[256,128]{1,0:T(8,128)(2,1)S(1)} %collective-permute-done.7.refs_2_, bf16[256,128]{1,0:T(8,128)(2,1)S(1)} %collective-permute-done.8.refs_3_, ...), custom_call_target="tpu_custom_call" | custom-call | tf_op jit(solution)/shard_map/join/pallas_call | solution.py:287
  (36 shorter events, 2.4 us)
Async XLA Ops:
  0.0 1.6 %copy-start = (bf16[8192,128]{1,0:T(8,128)(2,1)S(1)}, bf16[8192,128]{1,0:T(8,128)(2,1)}, u32[]{:S(2)}) copy-start(bf16[8192,128]{1,0:T(8,128)(2,1)} %donors.5) | copy-start | bytes 6291460
  1.6 1.6 %copy-start.2 = (bf16[1,1,8,8,128,128]{5,4,3,2,1,0:T(8,128)(2,1)S(1)}, bf16[1,1,8,8,128,128]{5,4,3,2,1,0:T(8,128)(2,1)}, u32[]{:S(2)}) copy-start(bf16[1,1,8,8,128,128]{5,4,3,2,1,0:T(8,128)(2,1)} %param.13) | copy-start | bytes 6291460
  3.2 0.7 %copy-start.5 = (s32[1,1,8,8]{3,2,1,0:T(8,128)S(1)}, s32[1,1,8,8]{3,2,1,0:T(8,128)}, u32[]{:S(2)}) copy-start(s32[1,1,8,8]{3,2,1,0:T(8,128)} %param.9) | copy-start | bytes 772
  6.4 19.3 %collective-permute-start.4 = (bf16[512,128]{1,0:T(8,128)(2,1)S(1)}, bf16[512,128]{1,0:T(8,128)(2,1)S(1)}, u32[]{:S(2)}, u32[]{:S(2)}) collective-permute-start(bf16[512,128]{1,0:T(8,128)(2,1)S(1)} %get-tuple-element.19), channel_id=1, source_target_pairs={{0,1},{1,0},{2,3},{3,2},{4,5},{5,4},{6,7},{7,6},{8,9},{9,8},{10,11... | collective-permute-start | bytes 393224 | tf_op jit(solution)/shard_map/ppermute | solution.py:23
  9.4 5.6 %copy-start.12 = (s32[1,1,8,2]{2,3,1,0:T(2,128)S(1)}, s32[1,1,8,2]{2,3,1,0:T(2,128)}, u32[]{:S(2)}) copy-start(s32[1,1,8,2]{2,3,1,0:T(2,128)} %param.12) | copy-start | bytes 196
  9.4 10.2 %copy-start.11 = (s32[1,1,1024]{2,1,0:T(1,128)S(1)}, s32[1,1,1024]{2,1,0:T(1,128)}, u32[]{:S(2)}) copy-start(s32[1,1,1024]{2,1,0:T(1,128)} %param.15) | copy-start | bytes 12292
  9.4 13.1 %copy-start.4 = (bf16[1,1,2,128,128]{4,3,2,1,0:T(8,128)(2,1)S(1)}, bf16[1,1,2,128,128]{4,3,2,1,0:T(8,128)(2,1)}, u32[]{:S(2)}) copy-start(bf16[1,1,2,128,128]{4,3,2,1,0:T(8,128)(2,1)} %param.14) | copy-start | bytes 196612
  9.4 16.2 %collective-permute-start.5 = (bf16[512,128]{1,0:T(8,128)(2,1)S(1)}, bf16[512,128]{1,0:T(8,128)(2,1)S(1)}, u32[]{:S(2)}, u32[]{:S(2)}) collective-permute-start(bf16[512,128]{1,0:T(8,128)(2,1)S(1)} %get-tuple-element.20), channel_id=1, source_target_pairs={{0,2},{1,3},{2,0},{3,1},{4,6},{5,7},{6,4},{7,5},{8,10},{9,11},{10,... | collective-permute-start | bytes 393224 | tf_op jit(solution)/shard_map/ppermute | solution.py:23
  11.0 12.6 %copy-start.3 = (bf16[1,1,8,8,128,128]{5,4,3,2,1,0:T(8,128)(2,1)S(1)}, bf16[1,1,8,8,128,128]{5,4,3,2,1,0:T(8,128)(2,1)}, u32[]{:S(2)}) copy-start(bf16[1,1,8,8,128,128]{5,4,3,2,1,0:T(8,128)(2,1)} %param.13) | copy-start | bytes 6291460
  13.5 10.2 %copy-start.1 = (bf16[8192,128]{1,0:T(8,128)(2,1)S(1)}, bf16[8192,128]{1,0:T(8,128)(2,1)}, u32[]{:S(2)}) copy-start(bf16[8192,128]{1,0:T(8,128)(2,1)} %donors.5) | copy-start | bytes 6291460
  13.5 10.2 %copy-start.6 = (s32[1,1,8,8]{3,2,1,0:T(8,128)S(1)}, s32[1,1,8,8]{3,2,1,0:T(8,128)}, u32[]{:S(2)}) copy-start(s32[1,1,8,8]{3,2,1,0:T(8,128)} %param.9) | copy-start | bytes 772
  13.5 10.2 %copy-start.8 = (s32[1,1,8,8]{3,2,1,0:T(8,128)S(1)}, s32[1,1,8,8]{3,2,1,0:T(8,128)}, u32[]{:S(2)}) copy-start(s32[1,1,8,8]{3,2,1,0:T(8,128)} %param.11) | copy-start | bytes 772
  13.5 10.2 %copy-start.10 = (s32[1,1,8]{2,1,0:T(1,128)S(1)}, s32[1,1,8]{2,1,0:T(1,128)}, u32[]{:S(2)}) copy-start(s32[1,1,8]{2,1,0:T(1,128)} %param.10) | copy-start | bytes 100
  13.5 12.1 %collective-permute-start.3 = (bf16[512,128]{1,0:T(8,128)(2,1)S(1)}, bf16[512,128]{1,0:T(8,128)(2,1)S(1)}, u32[]{:S(2)}, u32[]{:S(2)}) collective-permute-start(bf16[512,128]{1,0:T(8,128)(2,1)S(1)} %get-tuple-element.18), channel_id=1, source_target_pairs={{0,3},{1,2},{2,1},{3,0},{4,7},{5,6},{6,5},{7,4},{8,11},{9,10},{10,... | collective-permute-start | bytes 393224 | tf_op jit(solution)/shard_map/ppermute | solution.py:23
  13.6 12.0 %collective-permute-start.2 = (bf16[256,128]{1,0:T(8,128)(2,1)S(1)}, bf16[256,128]{1,0:T(8,128)(2,1)S(1)}, u32[]{:S(2)}, u32[]{:S(2)}) collective-permute-start(bf16[256,128]{1,0:T(8,128)(2,1)S(1)} %get-tuple-element.17), channel_id=1, source_target_pairs={{0,8},{8,16},{16,24},{1,9},{9,17},{17,25},{2,10},{10,18},{18,26},{... | collective-permute-start | bytes 196616 | tf_op jit(solution)/shard_map/ppermute | solution.py:326
  15.0 4.6 %collective-permute-start = (s32[2,8]{1,0:T(2,128)S(1)}, s32[2,8]{1,0:T(2,128)S(1)}, u32[]{:S(2)}, u32[]{:S(2)}) collective-permute-start(s32[2,8]{1,0:T(2,128)S(1)} %bitcast.24), channel_id=1, source_target_pairs={{0,4},{1,5},{2,6},{3,7},{4,0},{5,1},{6,2},{7,3},{8,12},{9,13},{10,... | collective-permute-start | bytes 200 | tf_op jit(solution)/shard_map/ppermute | solution.py:23
  19.6 5.1 %collective-permute-start.1 = (s32[8,128]{1,0:T(8,128)S(1)}, s32[8,128]{1,0:T(8,128)S(1)}, u32[]{:S(2)}, u32[]{:S(2)}) collective-permute-start(s32[8,128]{1,0:T(8,128)S(1)} %bitcast.22), channel_id=1, source_target_pairs={{0,4},{1,5},{2,6},{3,7},{4,0},{5,1},{6,2},{7,3},{8,12},{9,13},{10,... | collective-permute-start | bytes 12296 | tf_op jit(solution)/shard_map/ppermute | solution.py:23
  26.5 9.6 %collective-permute-start.10 = (bf16[256,128]{1,0:T(8,128)(2,1)S(1)}, bf16[256,128]{1,0:T(8,128)(2,1)S(1)}, u32[]{:S(2)}, u32[]{:S(2)}) collective-permute-start(bf16[256,128]{1,0:T(8,128)(2,1)S(1)} %get-tuple-element.26), channel_id=1, source_target_pairs={{0,5},{1,4},{2,7},{3,6},{4,1},{5,0},{6,3},{7,2},{8,13},{9,12},{10,... | collective-permute-start | bytes 196616 | tf_op jit(solution)/shard_map/ppermute | solution.py:23
  29.7 8.9 %collective-permute-start.11 = (bf16[256,128]{1,0:T(8,128)(2,1)S(1)}, bf16[256,128]{1,0:T(8,128)(2,1)S(1)}, u32[]{:S(2)}, u32[]{:S(2)}) collective-permute-start(bf16[256,128]{1,0:T(8,128)(2,1)S(1)} %get-tuple-element.27), channel_id=1, source_target_pairs={{0,6},{1,7},{2,4},{3,5},{4,2},{5,3},{6,0},{7,1},{8,14},{9,15},{10,... | collective-permute-start | bytes 196616 | tf_op jit(solution)/shard_map/ppermute | solution.py:23
  31.3 10.5 %collective-permute-start.12 = (bf16[256,128]{1,0:T(8,128)(2,1)S(1)}, bf16[256,128]{1,0:T(8,128)(2,1)S(1)}, u32[]{:S(2)}, u32[]{:S(2)}) collective-permute-start(bf16[256,128]{1,0:T(8,128)(2,1)S(1)} %get-tuple-element.28), channel_id=1, source_target_pairs={{0,7},{1,6},{2,5},{3,4},{4,3},{5,2},{6,1},{7,0},{8,15},{9,14},{10,... | collective-permute-start | bytes 196616 | tf_op jit(solution)/shard_map/ppermute | solution.py:23
  33.6 9.4 %collective-permute-start.9 = (bf16[256,128]{1,0:T(8,128)(2,1)S(1)}, bf16[256,128]{1,0:T(8,128)(2,1)S(1)}, u32[]{:S(2)}, u32[]{:S(2)}) collective-permute-start(bf16[256,128]{1,0:T(8,128)(2,1)S(1)} %get-tuple-element.25), channel_id=1, source_target_pairs={{0,4},{1,5},{2,6},{3,7},{4,0},{5,1},{6,2},{7,3},{8,12},{9,13},{10,... | collective-permute-start | bytes 196616 | tf_op jit(solution)/shard_map/ppermute | solution.py:23
  34.5 8.6 %collective-permute-start.6 = (bf16[256,128]{1,0:T(8,128)(2,1)S(1)}, bf16[256,128]{1,0:T(8,128)(2,1)S(1)}, u32[]{:S(2)}, u32[]{:S(2)}) collective-permute-start(bf16[256,128]{1,0:T(8,128)(2,1)S(1)} %get-tuple-element.22), channel_id=1, source_target_pairs={{0,1},{1,0},{2,3},{3,2},{4,5},{5,4},{6,7},{7,6},{8,9},{9,8},{10,11... | collective-permute-start | bytes 196616 | tf_op jit(solution)/shard_map/ppermute | solution.py:23
  36.1 6.9 %collective-permute-start.7 = (bf16[256,128]{1,0:T(8,128)(2,1)S(1)}, bf16[256,128]{1,0:T(8,128)(2,1)S(1)}, u32[]{:S(2)}, u32[]{:S(2)}) collective-permute-start(bf16[256,128]{1,0:T(8,128)(2,1)S(1)} %get-tuple-element.23), channel_id=1, source_target_pairs={{0,2},{1,3},{2,0},{3,1},{4,6},{5,7},{6,4},{7,5},{8,10},{9,11},{10,... | collective-permute-start | bytes 196616 | tf_op jit(solution)/shard_map/ppermute | solution.py:23
  38.6 6.4 %collective-permute-start.8 = (bf16[256,128]{1,0:T(8,128)(2,1)S(1)}, bf16[256,128]{1,0:T(8,128)(2,1)S(1)}, u32[]{:S(2)}, u32[]{:S(2)}) collective-permute-start(bf16[256,128]{1,0:T(8,128)(2,1)S(1)} %get-tuple-element.24), channel_id=1, source_target_pairs={{0,3},{1,2},{2,1},{3,0},{4,7},{5,6},{6,5},{7,4},{8,11},{9,10},{10,... | collective-permute-start | bytes 196616 | tf_op jit(solution)/shard_map/ppermute | solution.py:23
  (2 other events, 1.3 us)

commit v2 on v1

v2 whole, which is shorter than its diff:
```python
import functools

import jax
import jax.numpy as jnp
from jax import lax
from jax.experimental import pallas as pl
from jax.experimental.pallas import tpu as pltpu
from jax.sharding import PartitionSpec as P


VMEM = pl.BlockSpec(memory_space=pltpu.VMEM)
SMEM = pl.BlockSpec(memory_space=pltpu.SMEM)
HBM = pl.BlockSpec(memory_space=pltpu.HBM)
MARGIN = 4 << 20


def nbytes(*arrays):
    return sum(a.size * jnp.dtype(a.dtype).itemsize for a in arrays)


def swap(value, step):
    count = lax.axis_size("dom")
    return lax.ppermute(value, "dom", [(source, source ^ step) for source in range(count)])


def form_part(out, side, p, block_of, count_of, target_of, weight, block):
    capacity = block_of.shape[1]
    rows, width = weight(0).shape[0], out.shape[1]
    places = out.shape[0] // (2 * rows)
    pieces = []
    for k in range(capacity):
        value = block(k)
        live = k < count_of[p]
        kept = []
        for t in range(places):
            wanted = jnp.logical_and(live, target_of[p, k] == t)
            kept.append(jnp.where(wanted, value, jnp.zeros_like(value)))
        pieces.append(jnp.concatenate(kept, axis=1))
    total = jnp.dot(
        jnp.concatenate([weight(k) for k in range(capacity)], axis=1),
        jnp.concatenate(pieces, axis=0),
        preferred_element_type=jnp.float32,
    )
    for t in range(places):
        at = (side * places + t) * rows
        out[at : at + rows] = total[:, t * width : (t + 1) * width].astype(out.dtype)


def parts_kernel(steps, tables_hbm, order_hbm, table_hbm, donors, weights, *refs):
    outs = refs[: len(steps)]
    rim, packed = refs[len(steps) : len(steps) + 2]
    block_of, count_of, target_of, held_t, held_w, held_d, sems, sem_w = refs[len(steps) + 2 :]
    rows = held_w.shape[2]
    half = block_of.shape[0] // 2
    me = lax.axis_index("dom")
    owners = [(jnp.bitwise_xor(me, step), jnp.bitwise_xor(me, step + half)) for step in steps]
    copies = [
        pltpu.make_async_copy(source, target, sems.at[i])
        for i, (source, target) in enumerate(
            [
                *zip(tables_hbm, (block_of, count_of, target_of)),
                (donors, held_d),
                (order_hbm, packed.at[0 : order_hbm.shape[0]]),
                (table_hbm, held_t),
            ]
        )
    ]
    loads = [
        [
            pltpu.make_async_copy(weights.at[p], held_w.at[2 * i + j], sem_w.at[2 * i + j])
            for j, p in enumerate(pair)
        ]
        for i, pair in enumerate(owners)
    ]
    for copy in copies[:4] + sum(loads, []) + copies[4:]:
        copy.start()
    for copy in copies[:4] + sum(loads, []):
        copy.wait()
    for i, pair in enumerate(owners):
        for j, p in enumerate(pair):

            def block(c, p=p):
                row = pl.multiple_of(block_of[p, c] * rows, rows)
                return held_d[pl.ds(row, rows)]

            form_part(
                outs[i], j, p, block_of, count_of, target_of,
                lambda c, at=2 * i + j: held_w[at, c], block,
            )
    rim[...] = held_d[held_d.shape[0] - rim.shape[0] : held_d.shape[0]]
    for copy in copies[4:]:
        copy.wait()
    packed[order_hbm.shape[0] : order_hbm.shape[0] + held_t.shape[0], 0 : held_t.shape[1]] = (
        held_t[...]
    )


def form_parts(steps, tables, order, table, donors, weights, rim_rows):
    rows, width = weights.shape[2], donors.shape[1]
    places = table.shape[0]
    shapes = [jax.ShapeDtypeStruct((2 * places * rows, width), jnp.bfloat16)] * len(steps)
    shapes += [
        jax.ShapeDtypeStruct((rim_rows, width), donors.dtype),
        jax.ShapeDtypeStruct((order.shape[0] + 8, order.shape[1]), order.dtype),
    ]
    in_hbm = functools.partial(pltpu.with_memory_space_constraint, memory_space=pltpu.HBM)

    def kernel(block_hbm, count_hbm, target_hbm, *refs):
        parts_kernel(steps, (block_hbm, count_hbm, target_hbm), *refs)

    return pl.pallas_call(
        kernel,
        out_shape=shapes,
        in_specs=[HBM] * 7,
        out_specs=[VMEM] * len(shapes),
        scratch_shapes=[pltpu.SMEM(item.shape, item.dtype) for item in tables]
        + [
            pltpu.VMEM(table.shape, table.dtype),
            pltpu.VMEM(weights.shape, weights.dtype),
            pltpu.VMEM(donors.shape, donors.dtype),
            pltpu.SemaphoreType.DMA((6,)),
            pltpu.SemaphoreType.DMA((2 * len(steps),)),
        ],
        compiler_params=pltpu.CompilerParams(
            vmem_limit_bytes=nbytes(weights, donors, *shapes) + MARGIN
        ),
        cost_estimate=pl.CostEstimate(
            flops=4 * weights.size * width,
            bytes_accessed=nbytes(weights, donors),
            transcendentals=0,
        ),
        name="parts",
    )(*map(in_hbm, [*tables, order, table, donors, weights]))


def choose_kernel(steps, with_halo, places, packed, *refs):
    halo_w = refs[0] if with_halo else None
    chosen, place_of, sem = refs[-3:]
    blocks, rows = packed.shape[0] - place_of.shape[0], packed.shape[1]
    copy = pltpu.make_async_copy(packed.at[pl.ds(blocks, place_of.shape[0])], place_of, sem)
    copy.start()
    copy.wait()
    me = lax.axis_index("dom")
    lane = lax.broadcasted_iota(jnp.int32, (rows, rows), 1)
    starts = []
    for step in steps:
        q = jnp.bitwise_xor(me, step)
        starts += [place_of[t, q] * rows for t in range(places)]

    def fill(j, carry):
        wanted = (jnp.broadcast_to(packed[pl.ds(j, 1), :], (rows, rows)).T - lane).astype(jnp.int16)
        row = pl.multiple_of(j * rows, rows)
        for b, begin in enumerate(starts):
            chosen[pl.ds(row, rows), b * rows : (b + 1) * rows] = jnp.where(
                wanted == begin.astype(jnp.int16), jnp.bfloat16(1), jnp.bfloat16(0)
            )
        if with_halo:
            first = jnp.where(wanted == 0, jnp.bfloat16(1), jnp.bfloat16(0))
            both = jnp.concatenate([halo_w[h] for h in range(halo_w.shape[0])], axis=1)
            chosen[pl.ds(row, rows), len(starts) * rows :] = jnp.dot(
                first, both, preferred_element_type=jnp.float32
            ).astype(jnp.bfloat16)
        return carry

    for j in range(blocks):
        fill(j, 0)


def choose(steps, places, packed, halo_w=None):
    extra = [] if halo_w is None else [halo_w]
    blocks, rows = packed.shape[0] - 8, packed.shape[1]
    columns = len(steps) * places * rows + sum(h.shape[0] * h.shape[1] for h in extra)
    shape = jax.ShapeDtypeStruct((blocks * rows, columns), jnp.bfloat16)
    return pl.pallas_call(
        functools.partial(choose_kernel, steps, bool(extra), places),
        out_shape=shape,
        in_specs=[VMEM] * (1 + len(extra)),
        out_specs=VMEM,
        scratch_shapes=[pltpu.SMEM((8, rows), packed.dtype), pltpu.SemaphoreType.DMA(())],
        compiler_params=pltpu.CompilerParams(
            vmem_limit_bytes=nbytes(packed, shape, *extra) + MARGIN
        ),
        cost_estimate=pl.CostEstimate(
            flops=shape.size, bytes_accessed=nbytes(shape), transcendentals=0
        ),
        name="choose",
    )(packed, *extra)


def place_kernel(steps, far, share, own, other, rim, *refs):
    outs = refs[-1 - len(steps) : -1]
    parts = refs[: -1 - len(steps)]
    rows_of = refs[-1]
    me = lax.axis_index("dom")
    lot = len(steps) * share
    half = len(steps)
    begin = jnp.bitwise_xor(me // half, 1 if far else 0) * lot
    begin = pl.multiple_of(begin, lot)
    depth = parts[0].shape[0] // 2
    for side, matrix in enumerate((own, other)):
        stack = [part[side * depth : (side + 1) * depth] for part in parts]
        if side == 0:
            stack.append(rim[...])
        total = jnp.dot(
            matrix[pl.ds(begin, lot)],
            jnp.concatenate(stack, axis=0),
            preferred_element_type=jnp.float32,
        )
        rows_of[side] = total
    for step, out in zip(steps, outs):
        at = pl.multiple_of(lax.rem(jnp.bitwise_xor(me, step), half) * share, share)
        for side in range(2):
            out[side * share : (side + 1) * share] = rows_of[side, pl.ds(at, share)].astype(
                out.dtype
            )


def place(steps, far, share, own, other, rim, parts):
    width = rim.shape[1]
    shapes = [jax.ShapeDtypeStruct((2 * share, width), jnp.bfloat16)] * len(steps)
    held = jax.ShapeDtypeStruct((2, len(steps) * share, width), jnp.float32)
    return pl.pallas_call(
        functools.partial(place_kernel, steps, far, share),
        out_shape=shapes,
        in_specs=[VMEM] * (3 + len(parts)),
        out_specs=[VMEM] * len(shapes),
        scratch_shapes=[pltpu.VMEM(held.shape, held.dtype)],
        compiler_params=pltpu.CompilerParams(
            vmem_limit_bytes=nbytes(own, other, rim, held, *parts, *shapes) + MARGIN
        ),
        cost_estimate=pl.CostEstimate(
            flops=own.size * width * 2, bytes_accessed=nbytes(own), transcendentals=0
        ),
        name="place",
    )(own, other, rim, *parts)


def join_kernel(count, *refs):
    chunks = refs[:count]
    out, held, sem = refs[count:]
    share = chunks[0].shape[0] // 2
    me = lax.axis_index("dom")
    copies = []
    for step in range(count):
        row = pl.multiple_of(jnp.bitwise_xor(me, step) * share, share)
        pair = chunks[step ^ (count // 2)]
        total = chunks[step][:share].astype(jnp.float32) + pair[share:].astype(jnp.float32)
        held[step] = total.astype(held.dtype)
        copies.append(pltpu.make_async_copy(held.at[step], out.at[pl.ds(row, share)], sem.at[step]))
        copies[-1].start()
    for copy in copies:
        copy.wait()


def join(chunks):
    count = len(chunks)
    share, width = chunks[0].shape[0] // 2, chunks[0].shape[1]
    return pl.pallas_call(
        functools.partial(join_kernel, count),
        out_shape=jax.ShapeDtypeStruct((share * count, width), chunks[0].dtype),
        in_specs=[VMEM] * count,
        out_specs=HBM,
        scratch_shapes=[
            pltpu.VMEM((count, share, width), chunks[0].dtype),
            pltpu.SemaphoreType.DMA((count,)),
        ],
        compiler_params=pltpu.CompilerParams(vmem_limit_bytes=2 * nbytes(*chunks) + MARGIN),
        name="join",
    )(*chunks)


def near_steps(count):
    half = count // 2
    return list(range(1, half))


def on_device(
    donors, send_block, send_count, send_target, target_block, weights, halo_weights, permute
):
    block_rows = weights.shape[-1]
    rim_rows = halo_weights.shape[2] * block_rows
    count = lax.axis_size("dom")
    slabs = lax.axis_size("slab")
    half = count // 2
    share = permute.shape[-1] // count
    tables = send_block[0, 0], send_count[0, 0], send_target[0, 0]
    places = target_block.shape[-1]
    near = near_steps(count)
    order = permute[0, 0].reshape(-1, block_rows)
    *formed, own_part, rim, packed = form_parts(
        near + [0], tables, order, target_block[0, 0].T, donors, weights[0, 0], rim_rows
    )
    arrived = [swap(part, step) for part, step in zip(formed, near)]
    other_packed = swap(packed, half)
    rim = lax.ppermute(rim, "slab", [(source, source + 1) for source in range(slabs - 1)])
    own = choose([0] + near, places, packed, halo_weights[0, 0])
    other = choose([0] + near, places, other_packed)
    parts = [own_part, *arrived]
    far_steps = list(range(half, count))
    far = place(far_steps, True, share, own, other, rim, parts)
    close_steps = list(range(1, half)) + [0]
    close = place(close_steps, False, share, own, other, rim, parts)
    chunks = [None] * count
    chunks[0] = close[-1]
    for step, chunk in zip(far_steps + close_steps[:-1], far + close[:-1]):
        chunks[step] = swap(chunk, step)
    return join(chunks)


def solution(mesh):
    return jax.shard_map(
        on_device,
        mesh=mesh,
        in_specs=(
            P(("slab", "dom"), None),
            P("slab", "dom", None, None),
            P("slab", "dom", None),
            P("slab", "dom", None, None),
            P("slab", "dom", None, None),
            P("slab", "dom", None, None, None, None),
            P("slab", "dom", None, None, None),
            P("slab", "dom", None),
        ),
        out_specs=P(("slab", "dom"), None),
        check_vma=False,
    )
```

time: 46.1 us -> 35 us (0.76)
  local copies, waits for them, and re-layouts: 5.25 us -> 0.01 us
  starting transfers between devices: 26.3 us -> 21.9 us
  Pallas kernels: 9.02 us -> 7.62 us
    unnamed x26 -> x2, local copies, waits for them, and re-layouts: 5.25 us -> 0.01 us
    ppermute x12 -> x11, starting transfers between devices: 24.9 us -> 20.6 us  [swap(): lax.ppermute(value, 'dom', [(source, source ^ step) for source in range(c...]
    pallas_call x5 -> x3, Pallas kernels: 6.6 us -> 5.21 us  [the longest x1 3.07 us: form_parts(): pl.pallas_call(kernel, out_shape=shapes, in_specs=[HBM] * 7, out_specs=[V...]
    ppermute x12 -> x11, waiting for transfers between devices: 4.97 us -> 5.25 us  [swap(): lax.ppermute(value, 'dom', [(source, source ^ step) for source in range(c...]
  transfers between devices with their start and end apart: 13 -> 12, of which waited for: 4 -> 5; matrix products, arithmetic and copies ran while one was open for 0% -> 0% of each run, Pallas kernels for 14% -> 9%
where the time goes in v2:
time: 35 us; the launch traced here: 34.8 us
  starting transfers between devices  21.9 us (63%)
  Pallas kernels  7.62 us (22%)
  waiting for transfers between devices  5.26 us (15%)
    ppermute x11, starting transfers between devices, swap(): lax.ppermute(value, 'dom', [(source, source ^ step) for source in range(c...  20.6 us
    ppermute x11, waiting for transfers between devices, swap(): lax.ppermute(value, 'dom', [(source, source ^ step) for source in range(c...  5.25 us
    pallas_call x1, Pallas kernels, form_parts(): pl.pallas_call(kernel, out_shape=shapes, in_specs=[HBM] * 7, out_specs=[V...  3.07 us
    pallas_call x2, Pallas kernels, choose(): pl.pallas_call(functools.partial(choose_kernel, steps, bool(extra), place...  2.14 us
    pallas_call x2, Pallas kernels, place(): pl.pallas_call(functools.partial(place_kernel, steps, far, share), out_sh...  1.65 us
    ppermute x1, starting transfers between devices, on_device(): lax.ppermute(rim, 'slab', [(source, source + 1) for source in range(slabs...  1.28 us
    pallas_call x1, Pallas kernels, join(): pl.pallas_call(functools.partial(join_kernel, count), out_shape=jax.Shape...  0.77 us
  transfers between devices with their start and end apart: 12, of which 5 were waited for; matrix products, arithmetic and copies ran while one was open for 0% of the time, Pallas kernels for 9%

profile of v2, /device:TPU:0, one launch (start us, length us, event | category | flops | bytes accessed | tf_op | source)
XLA Modules:
  0.0 34.8 jit_solution(603571675375767817)
XLA Ops:
  0.0 3.1 %parts.1 = (bf16[512,128]{1,0:T(8,128)(2,1)S(1)}, bf16[512,128]{1,0:T(8,128)(2,1)S(1)}, bf16[512,128]{1,0:T(8,128)(2,1)S(1)}, bf16[512,128]{1,0:T(8,128)(2,1)S(1...) custom-call(s32[8,8]{1,0:T(8,128)} %bitcast.11, s32[8]{0:T(128)} %bitcast.15, s32[8,8]{1,0:T(8,128)} %bitcast.12, ...), custom_call_target="tpu_custom_call" | custom-call | flops 536870912 | bytes 4194304 | tf_op jit(solution)/shard_map/parts/pallas_call | solution.py:111
  3.1 3.1 %collective-permute-start.2 = (bf16[512,128]{1,0:T(8,128)(2,1)S(1)}, bf16[512,128]{1,0:T(8,128)(2,1)S(1)}, u32[]{:S(2)}, u32[]{:S(2)}) collective-permute-start(bf16[512,128]{1,0:T(8,128)(2,1)S(1)} %get-tuple-element.22), channel_id=1, source_target_pairs={{0,1},{1,0},{2,3},{3,2},{4,5},{5,4},{6,7},{7,6},{8,9},{9,8},{10,11... | collective-permute-start | bytes 393224 | tf_op jit(solution)/shard_map/ppermute | solution.py:23
  6.1 1.6 %collective-permute-start.3 = (bf16[512,128]{1,0:T(8,128)(2,1)S(1)}, bf16[512,128]{1,0:T(8,128)(2,1)S(1)}, u32[]{:S(2)}, u32[]{:S(2)}) collective-permute-start(bf16[512,128]{1,0:T(8,128)(2,1)S(1)} %get-tuple-element.23), channel_id=1, source_target_pairs={{0,2},{1,3},{2,0},{3,1},{4,6},{5,7},{6,4},{7,5},{8,10},{9,11},{10,... | collective-permute-start | bytes 393224 | tf_op jit(solution)/shard_map/ppermute | solution.py:23
  7.7 0.0 collective-permute-start.4
  7.7 1.3 %collective-permute-start.1 = (bf16[256,128]{1,0:T(8,128)(2,1)S(1)}, bf16[256,128]{1,0:T(8,128)(2,1)S(1)}, u32[]{:S(2)}, u32[]{:S(2)}) collective-permute-start(bf16[256,128]{1,0:T(8,128)(2,1)S(1)} %get-tuple-element.20), channel_id=1, source_target_pairs={{0,8},{8,16},{16,24},{1,9},{9,17},{17,25},{2,10},{10,18},{18,26},{... | collective-permute-start | bytes 196616 | tf_op jit(solution)/shard_map/ppermute | solution.py:295
  9.0 3.0 %collective-permute-start = (s32[16,128]{1,0:T(8,128)S(1)}, s32[16,128]{1,0:T(8,128)S(1)}, u32[]{:S(2)}, u32[]{:S(2)}) collective-permute-start(s32[16,128]{1,0:T(8,128)S(1)} %get-tuple-element.19.packed), channel_id=1, source_target_pairs={{0,4},{1,5},{2,6},{3,7},{4,0},{5,1},{6,2},{7,3},{8,12},{9,13},{10,... | collective-permute-start | bytes 24584 | tf_op jit(solution)/shard_map/ppermute | solution.py:23
  12.1 1.1 %choose.2.own = bf16[1024,1280]{1,0:T(8,128)(2,1)S(1)} custom-call(s32[16,128]{1,0:T(8,128)S(1)} %get-tuple-element.19.packed, bf16[2,128,128]{2,1,0:T(8,128)(2,1)S(1)} %bitcast.9), custom_call_target="tpu_custom_call" | custom-call | flops 1310720 | bytes 2621440 | tf_op jit(solution)/shard_map/choose/pallas_call | solution.py:174
  13.2 0.6 %collective-permute-done.packed = s32[16,128]{1,0:T(8,128)S(1)} collective-permute-done((s32[16,128]{1,0:T(8,128)S(1)}, s32[16,128]{1,0:T(8,128)S(1)}, u32[]{:S(2)}, u32[]{:S(2)}) %collective-permute-start) | collective-permute-done | bytes 8224 | tf_op jit(solution)/shard_map/ppermute | solution.py:23
  13.8 1.0 %choose.3.other = bf16[1024,1024]{1,0:T(8,128)(2,1)S(1)} custom-call(s32[16,128]{1,0:T(8,128)S(1)} %collective-permute-done.packed), custom_call_target="tpu_custom_call" | custom-call | flops 1048576 | bytes 2097152 | tf_op jit(solution)/shard_map/choose/pallas_call | solution.py:174
  14.8 0.0 collective-permute-done.1.rim
  14.8 0.8 %place.3 = (bf16[256,128]{1,0:T(8,128)(2,1)S(1)}, bf16[256,128]{1,0:T(8,128)(2,1)S(1)}, bf16[256,128]{1,0:T(8,128)(2,1)S(1)}, bf16[256,128]{1,0:T(8,128)(2,1)S(1)}) custom-call(bf16[1024,1280]{1,0:T(8,128)(2,1)S(1)} %choose.2.own, bf16[1024,1024]{1,0:T(8,128)(2,1)S(1)} %choose.3.other, bf16[256,128]{1,0:T(8,128)(2,1)S(1)} %collective-permute-done.1.rim, ...), custom_call_target="tpu_custom_call" | custom-call | flops 335544320 | bytes 2621440 | tf_op jit(solution)/shard_map/place/pallas_call | solution.py:222
  15.7 3.9 %collective-permute-start.10 = (bf16[256,128]{1,0:T(8,128)(2,1)S(1)}, bf16[256,128]{1,0:T(8,128)(2,1)S(1)}, u32[]{:S(2)}, u32[]{:S(2)}) collective-permute-start(bf16[256,128]{1,0:T(8,128)(2,1)S(1)} %get-tuple-element.31), channel_id=1, source_target_pairs={{0,6},{1,7},{2,4},{3,5},{4,2},{5,3},{6,0},{7,1},{8,14},{9,15},{10,... | collective-permute-start | bytes 196616 | tf_op jit(solution)/shard_map/ppermute | solution.py:23
  19.6 1.2 %collective-permute-start.11 = (bf16[256,128]{1,0:T(8,128)(2,1)S(1)}, bf16[256,128]{1,0:T(8,128)(2,1)S(1)}, u32[]{:S(2)}, u32[]{:S(2)}) collective-permute-start(bf16[256,128]{1,0:T(8,128)(2,1)S(1)} %get-tuple-element.32), channel_id=1, source_target_pairs={{0,7},{1,6},{2,5},{3,4},{4,3},{5,2},{6,1},{7,0},{8,15},{9,14},{10,... | collective-permute-start | bytes 196616 | tf_op jit(solution)/shard_map/ppermute | solution.py:23
  20.7 0.8 %collective-permute-start.8 = (bf16[256,128]{1,0:T(8,128)(2,1)S(1)}, bf16[256,128]{1,0:T(8,128)(2,1)S(1)}, u32[]{:S(2)}, u32[]{:S(2)}) collective-permute-start(bf16[256,128]{1,0:T(8,128)(2,1)S(1)} %get-tuple-element.29), channel_id=1, source_target_pairs={{0,4},{1,5},{2,6},{3,7},{4,0},{5,1},{6,2},{7,3},{8,12},{9,13},{10,... | collective-permute-start | bytes 196616 | tf_op jit(solution)/shard_map/ppermute | solution.py:23
  21.5 1.9 %collective-permute-start.9 = (bf16[256,128]{1,0:T(8,128)(2,1)S(1)}, bf16[256,128]{1,0:T(8,128)(2,1)S(1)}, u32[]{:S(2)}, u32[]{:S(2)}) collective-permute-start(bf16[256,128]{1,0:T(8,128)(2,1)S(1)} %get-tuple-element.30), channel_id=1, source_target_pairs={{0,5},{1,4},{2,7},{3,6},{4,1},{5,0},{6,3},{7,2},{8,13},{9,12},{10,... | collective-permute-start | bytes 196616 | tf_op jit(solution)/shard_map/ppermute | solution.py:23
  23.5 0.8 %place.2 = (bf16[256,128]{1,0:T(8,128)(2,1)S(1)}, bf16[256,128]{1,0:T(8,128)(2,1)S(1)}, bf16[256,128]{1,0:T(8,128)(2,1)S(1)}, bf16[256,128]{1,0:T(8,128)(2,1)S(1)}) custom-call(bf16[1024,1280]{1,0:T(8,128)(2,1)S(1)} %choose.2.own, bf16[1024,1024]{1,0:T(8,128)(2,1)S(1)} %choose.3.other, bf16[256,128]{1,0:T(8,128)(2,1)S(1)} %collective-permute-done.1.rim, ...), custom_call_target="tpu_custom_call" | custom-call | flops 335544320 | bytes 2621440 | tf_op jit(solution)/shard_map/place/pallas_call | solution.py:222
  24.3 1.7 %collective-permute-start.5 = (bf16[256,128]{1,0:T(8,128)(2,1)S(1)}, bf16[256,128]{1,0:T(8,128)(2,1)S(1)}, u32[]{:S(2)}, u32[]{:S(2)}) collective-permute-start(bf16[256,128]{1,0:T(8,128)(2,1)S(1)} %get-tuple-element.26), channel_id=1, source_target_pairs={{0,1},{1,0},{2,3},{3,2},{4,5},{5,4},{6,7},{7,6},{8,9},{9,8},{10,11... | collective-permute-start | bytes 196616 | tf_op jit(solution)/shard_map/ppermute | solution.py:23
  26.0 1.2 %collective-permute-start.6 = (bf16[256,128]{1,0:T(8,128)(2,1)S(1)}, bf16[256,128]{1,0:T(8,128)(2,1)S(1)}, u32[]{:S(2)}, u32[]{:S(2)}) collective-permute-start(bf16[256,128]{1,0:T(8,128)(2,1)S(1)} %get-tuple-element.27), channel_id=1, source_target_pairs={{0,2},{1,3},{2,0},{3,1},{4,6},{5,7},{6,4},{7,5},{8,10},{9,11},{10,... | collective-permute-start | bytes 196616 | tf_op jit(solution)/shard_map/ppermute | solution.py:23
  27.3 0.1 collective-permute-done.11.refs_7_
  27.3 2.1 %collective-permute-start.7 = (bf16[256,128]{1,0:T(8,128)(2,1)S(1)}, bf16[256,128]{1,0:T(8,128)(2,1)S(1)}, u32[]{:S(2)}, u32[]{:S(2)}) collective-permute-start(bf16[256,128]{1,0:T(8,128)(2,1)S(1)} %get-tuple-element.28), channel_id=1, source_target_pairs={{0,3},{1,2},{2,1},{3,0},{4,7},{5,6},{6,5},{7,4},{8,11},{9,10},{10,... | collective-permute-start | bytes 196616 | tf_op jit(solution)/shard_map/ppermute | solution.py:23
  29.5 1.4 %collective-permute-done.8.refs_4_ = bf16[256,128]{1,0:T(8,128)(2,1)S(1)} collective-permute-done((bf16[256,128]{1,0:T(8,128)(2,1)S(1)}, bf16[256,128]{1,0:T(8,128)(2,1)S(1)}, u32[]{:S(2)}, u32[]{:S(2)}) %collective-permute-start.8) | collective-permute-done | bytes 65568 | tf_op jit(solution)/shard_map/ppermute | solution.py:23
  30.8 1.7 %collective-permute-done.9.refs_5_ = bf16[256,128]{1,0:T(8,128)(2,1)S(1)} collective-permute-done((bf16[256,128]{1,0:T(8,128)(2,1)S(1)}, bf16[256,128]{1,0:T(8,128)(2,1)S(1)}, u32[]{:S(2)}, u32[]{:S(2)}) %collective-permute-start.9) | collective-permute-done | bytes 65568 | tf_op jit(solution)/shard_map/ppermute | solution.py:23
  32.5 1.5 %collective-permute-done.7.refs_3_ = bf16[256,128]{1,0:T(8,128)(2,1)S(1)} collective-permute-done((bf16[256,128]{1,0:T(8,128)(2,1)S(1)}, bf16[256,128]{1,0:T(8,128)(2,1)S(1)}, u32[]{:S(2)}, u32[]{:S(2)}) %collective-permute-start.7) | collective-permute-done | bytes 65568 | tf_op jit(solution)/shard_map/ppermute | solution.py:23
  34.1 0.8 %join.1 = bf16[1024,128]{1,0:T(8,128)(2,1)} custom-call(bf16[256,128]{1,0:T(8,128)(2,1)S(1)} %get-tuple-element.25.refs_0_, bf16[256,128]{1,0:T(8,128)(2,1)S(1)} %collective-permute-done.5.refs_1_, bf16[256,128]{1,0:T(8,128)(2,1)S(1)} %collective-permute-done.6.refs_2_, bf16[256,128]{1,0:T(8,128)(2,1)S(1)} %collective-permute-done.7.refs_3_, ...), custom_call_target="tpu_custom_call" | custom-call | tf_op jit(solution)/shard_map/join/pallas_call | solution.py:258
  (8 shorter events, 0.0 us)
Async XLA Ops:
  0.0 12.1 %copy-start = (bf16[1,1,2,128,128]{4,3,2,1,0:T(8,128)(2,1)S(1)}, bf16[1,1,2,128,128]{4,3,2,1,0:T(8,128)(2,1)}, u32[]{:S(2)}) copy-start(bf16[1,1,2,128,128]{4,3,2,1,0:T(8,128)(2,1)} %param.14) | copy-start | bytes 196612
  3.1 11.7 %collective-permute-start.2 = (bf16[512,128]{1,0:T(8,128)(2,1)S(1)}, bf16[512,128]{1,0:T(8,128)(2,1)S(1)}, u32[]{:S(2)}, u32[]{:S(2)}) collective-permute-start(bf16[512,128]{1,0:T(8,128)(2,1)S(1)} %get-tuple-element.22), channel_id=1, source_target_pairs={{0,1},{1,0},{2,3},{3,2},{4,5},{5,4},{6,7},{7,6},{8,9},{9,8},{10,11... | collective-permute-start | bytes 393224 | tf_op jit(solution)/shard_map/ppermute | solution.py:23
  6.1 8.7 %collective-permute-start.3 = (bf16[512,128]{1,0:T(8,128)(2,1)S(1)}, bf16[512,128]{1,0:T(8,128)(2,1)S(1)}, u32[]{:S(2)}, u32[]{:S(2)}) collective-permute-start(bf16[512,128]{1,0:T(8,128)(2,1)S(1)} %get-tuple-element.23), channel_id=1, source_target_pairs={{0,2},{1,3},{2,0},{3,1},{4,6},{5,7},{6,4},{7,5},{8,10},{9,11},{10,... | collective-permute-start | bytes 393224 | tf_op jit(solution)/shard_map/ppermute | solution.py:23
  7.7 7.1 %collective-permute-start.4 = (bf16[512,128]{1,0:T(8,128)(2,1)S(1)}, bf16[512,128]{1,0:T(8,128)(2,1)S(1)}, u32[]{:S(2)}, u32[]{:S(2)}) collective-permute-start(bf16[512,128]{1,0:T(8,128)(2,1)S(1)} %get-tuple-element.24), channel_id=1, source_target_pairs={{0,3},{1,2},{2,1},{3,0},{4,7},{5,6},{6,5},{7,4},{8,11},{9,10},{10,... | collective-permute-start | bytes 393224 | tf_op jit(solution)/shard_map/ppermute | solution.py:23
  7.7 7.1 %collective-permute-start.1 = (bf16[256,128]{1,0:T(8,128)(2,1)S(1)}, bf16[256,128]{1,0:T(8,128)(2,1)S(1)}, u32[]{:S(2)}, u32[]{:S(2)}) collective-permute-start(bf16[256,128]{1,0:T(8,128)(2,1)S(1)} %get-tuple-element.20), channel_id=1, source_target_pairs={{0,8},{8,16},{16,24},{1,9},{9,17},{17,25},{2,10},{10,18},{18,26},{... | collective-permute-start | bytes 196616 | tf_op jit(solution)/shard_map/ppermute | solution.py:295
  9.0 4.8 %collective-permute-start = (s32[16,128]{1,0:T(8,128)S(1)}, s32[16,128]{1,0:T(8,128)S(1)}, u32[]{:S(2)}, u32[]{:S(2)}) collective-permute-start(s32[16,128]{1,0:T(8,128)S(1)} %get-tuple-element.19.packed), channel_id=1, source_target_pairs={{0,4},{1,5},{2,6},{3,7},{4,0},{5,1},{6,2},{7,3},{8,12},{9,13},{10,... | collective-permute-start | bytes 24584 | tf_op jit(solution)/shard_map/ppermute | solution.py:23
  15.7 10.4 %collective-permute-start.10 = (bf16[256,128]{1,0:T(8,128)(2,1)S(1)}, bf16[256,128]{1,0:T(8,128)(2,1)S(1)}, u32[]{:S(2)}, u32[]{:S(2)}) collective-permute-start(bf16[256,128]{1,0:T(8,128)(2,1)S(1)} %get-tuple-element.31), channel_id=1, source_target_pairs={{0,6},{1,7},{2,4},{3,5},{4,2},{5,3},{6,0},{7,1},{8,14},{9,15},{10,... | collective-permute-start | bytes 196616 | tf_op jit(solution)/shard_map/ppermute | solution.py:23
  19.6 7.8 %collective-permute-start.11 = (bf16[256,128]{1,0:T(8,128)(2,1)S(1)}, bf16[256,128]{1,0:T(8,128)(2,1)S(1)}, u32[]{:S(2)}, u32[]{:S(2)}) collective-permute-start(bf16[256,128]{1,0:T(8,128)(2,1)S(1)} %get-tuple-element.32), channel_id=1, source_target_pairs={{0,7},{1,6},{2,5},{3,4},{4,3},{5,2},{6,1},{7,0},{8,15},{9,14},{10,... | collective-permute-start | bytes 196616 | tf_op jit(solution)/shard_map/ppermute | solution.py:23
  20.7 10.1 %collective-permute-start.8 = (bf16[256,128]{1,0:T(8,128)(2,1)S(1)}, bf16[256,128]{1,0:T(8,128)(2,1)S(1)}, u32[]{:S(2)}, u32[]{:S(2)}) collective-permute-start(bf16[256,128]{1,0:T(8,128)(2,1)S(1)} %get-tuple-element.29), channel_id=1, source_target_pairs={{0,4},{1,5},{2,6},{3,7},{4,0},{5,1},{6,2},{7,3},{8,12},{9,13},{10,... | collective-permute-start | bytes 196616 | tf_op jit(solution)/shard_map/ppermute | solution.py:23
  21.5 11.0 %collective-permute-start.9 = (bf16[256,128]{1,0:T(8,128)(2,1)S(1)}, bf16[256,128]{1,0:T(8,128)(2,1)S(1)}, u32[]{:S(2)}, u32[]{:S(2)}) collective-permute-start(bf16[256,128]{1,0:T(8,128)(2,1)S(1)} %get-tuple-element.30), channel_id=1, source_target_pairs={{0,5},{1,4},{2,7},{3,6},{4,1},{5,0},{6,3},{7,2},{8,13},{9,12},{10,... | collective-permute-start | bytes 196616 | tf_op jit(solution)/shard_map/ppermute | solution.py:23
  24.3 8.3 %collective-permute-start.5 = (bf16[256,128]{1,0:T(8,128)(2,1)S(1)}, bf16[256,128]{1,0:T(8,128)(2,1)S(1)}, u32[]{:S(2)}, u32[]{:S(2)}) collective-permute-start(bf16[256,128]{1,0:T(8,128)(2,1)S(1)} %get-tuple-element.26), channel_id=1, source_target_pairs={{0,1},{1,0},{2,3},{3,2},{4,5},{5,4},{6,7},{7,6},{8,9},{9,8},{10,11... | collective-permute-start | bytes 196616 | tf_op jit(solution)/shard_map/ppermute | solution.py:23
  26.0 6.5 %collective-permute-start.6 = (bf16[256,128]{1,0:T(8,128)(2,1)S(1)}, bf16[256,128]{1,0:T(8,128)(2,1)S(1)}, u32[]{:S(2)}, u32[]{:S(2)}) collective-permute-start(bf16[256,128]{1,0:T(8,128)(2,1)S(1)} %get-tuple-element.27), channel_id=1, source_target_pairs={{0,2},{1,3},{2,0},{3,1},{4,6},{5,7},{6,4},{7,5},{8,10},{9,11},{10,... | collective-permute-start | bytes 196616 | tf_op jit(solution)/shard_map/ppermute | solution.py:23
  27.3 6.7 %collective-permute-start.7 = (bf16[256,128]{1,0:T(8,128)(2,1)S(1)}, bf16[256,128]{1,0:T(8,128)(2,1)S(1)}, u32[]{:S(2)}, u32[]{:S(2)}) collective-permute-start(bf16[256,128]{1,0:T(8,128)(2,1)S(1)} %get-tuple-element.28), channel_id=1, source_target_pairs={{0,3},{1,2},{2,1},{3,0},{4,7},{5,6},{6,5},{7,4},{8,11},{9,10},{10,... | collective-permute-start | bytes 196616 | tf_op jit(solution)/shard_map/ppermute | solution.py:23

commit v3 on v2

--- a/solution.py
+++ b/solution.py
@@ -135,24 +135,25 @@
 
 def choose_kernel(steps, with_halo, places, packed, *refs):
     halo_w = refs[0] if with_halo else None
-    chosen, place_of, sem = refs[-3:]
-    blocks, rows = packed.shape[0] - place_of.shape[0], packed.shape[1]
-    copy = pltpu.make_async_copy(packed.at[pl.ds(blocks, place_of.shape[0])], place_of, sem)
-    copy.start()
-    copy.wait()
+    chosen = refs[-1]
+    blocks, rows = packed.shape[0] - 8, packed.shape[1]
+    column = lax.broadcasted_iota(jnp.int32, (1, rows), 1)
     me = lax.axis_index("dom")
     lane = lax.broadcasted_iota(jnp.int32, (rows, rows), 1)
     starts = []
     for step in steps:
         q = jnp.bitwise_xor(me, step)
-        starts += [place_of[t, q] * rows for t in range(places)]
+        for t in range(places):
+            table = packed[blocks + t : blocks + t + 1]
+            place = jnp.sum(jnp.where(column == q, table, 0), axis=1, keepdims=True)
+            starts.append(jnp.broadcast_to(place * rows, (rows, rows)).astype(jnp.int16))
 
     def fill(j, carry):
         wanted = (jnp.broadcast_to(packed[pl.ds(j, 1), :], (rows, rows)).T - lane).astype(jnp.int16)
         row = pl.multiple_of(j * rows, rows)
         for b, begin in enumerate(starts):
             chosen[pl.ds(row, rows), b * rows : (b + 1) * rows] = jnp.where(
-                wanted == begin.astype(jnp.int16), jnp.bfloat16(1), jnp.bfloat16(0)
+                wanted == begin, jnp.bfloat16(1), jnp.bfloat16(0)
             )
         if with_halo:
             first = jnp.where(wanted == 0, jnp.bfloat16(1), jnp.bfloat16(0))
@@ -176,7 +177,6 @@
         out_shape=shape,
         in_specs=[VMEM] * (1 + len(extra)),
         out_specs=VMEM,
-        scratch_shapes=[pltpu.SMEM((8, rows), packed.dtype), pltpu.SemaphoreType.DMA(())],
         compiler_params=pltpu.CompilerParams(
             vmem_limit_bytes=nbytes(packed, shape, *extra) + MARGIN
         ),

time: 35 us -> 34.4 us (0.983)
  Pallas kernels: 7.62 us -> 6.55 us
  waiting for transfers between devices: 5.26 us -> 5.77 us
    pallas_call x2, Pallas kernels: 2.14 us -> 1.06 us  [choose(): pl.pallas_call(functools.partial(choose_kernel, steps, bool(extra), place...]
    ppermute x11, waiting for transfers between devices: 5.25 us -> 5.77 us  [swap(): lax.ppermute(value, 'dom', [(source, source ^ step) for source in range(c...]
  transfers between devices with their start and end apart: 12 -> 12, of which waited for: 5 -> 5; matrix products, arithmetic and copies ran while one was open for 0% -> 0% of each run, Pallas kernels for 9% -> 6%
where the time goes in v3:
time: 34.4 us; the launch traced here: 34.3 us
  starting transfers between devices  21.9 us (64%)
  Pallas kernels  6.55 us (19%)
  waiting for transfers between devices  5.77 us (17%)
    ppermute x11, starting transfers between devices, swap(): lax.ppermute(value, 'dom', [(source, source ^ step) for source in range(c...  20.6 us
    ppermute x11, waiting for transfers between devices, swap(): lax.ppermute(value, 'dom', [(source, source ^ step) for source in range(c...  5.77 us
    pallas_call x1, Pallas kernels, form_parts(): pl.pallas_call(kernel, out_shape=shapes, in_specs=[HBM] * 7, out_specs=[V...  3.07 us
    pallas_call x2, Pallas kernels, place(): pl.pallas_call(functools.partial(place_kernel, steps, far, share), out_sh...  1.65 us
    ppermute x1, starting transfers between devices, on_device(): lax.ppermute(rim, 'slab', [(source, source + 1) for source in range(slabs...  1.28 us
    pallas_call x2, Pallas kernels, choose(): pl.pallas_call(functools.partial(choose_kernel, steps, bool(extra), place...  1.06 us
    pallas_call x1, Pallas kernels, join(): pl.pallas_call(functools.partial(join_kernel, count), out_shape=jax.Shape...  0.77 us
  transfers between devices with their start and end apart: 12, of which 5 were waited for; matrix products, arithmetic and copies ran while one was open for 0% of the time, Pallas kernels for 6%

profile of v3, /device:TPU:0, one launch (start us, length us, event | category | flops | bytes accessed | tf_op | source)
XLA Modules:
  0.0 34.3 jit_solution(8559960625441892350)
XLA Ops:
  0.0 3.1 %parts.1 = (bf16[512,128]{1,0:T(8,128)(2,1)S(1)}, bf16[512,128]{1,0:T(8,128)(2,1)S(1)}, bf16[512,128]{1,0:T(8,128)(2,1)S(1)}, bf16[512,128]{1,0:T(8,128)(2,1)S(1...) custom-call(s32[8,8]{1,0:T(8,128)} %bitcast.11, s32[8]{0:T(128)} %bitcast.15, s32[8,8]{1,0:T(8,128)} %bitcast.12, ...), custom_call_target="tpu_custom_call" | custom-call | flops 536870912 | bytes 4194304 | tf_op jit(solution)/shard_map/parts/pallas_call | solution.py:111
  3.1 3.1 %collective-permute-start.2 = (bf16[512,128]{1,0:T(8,128)(2,1)S(1)}, bf16[512,128]{1,0:T(8,128)(2,1)S(1)}, u32[]{:S(2)}, u32[]{:S(2)}) collective-permute-start(bf16[512,128]{1,0:T(8,128)(2,1)S(1)} %get-tuple-element.22), channel_id=1, source_target_pairs={{0,1},{1,0},{2,3},{3,2},{4,5},{5,4},{6,7},{7,6},{8,9},{9,8},{10,11... | collective-permute-start | bytes 393224 | tf_op jit(solution)/shard_map/ppermute | solution.py:23
  6.1 1.6 %collective-permute-start.3 = (bf16[512,128]{1,0:T(8,128)(2,1)S(1)}, bf16[512,128]{1,0:T(8,128)(2,1)S(1)}, u32[]{:S(2)}, u32[]{:S(2)}) collective-permute-start(bf16[512,128]{1,0:T(8,128)(2,1)S(1)} %get-tuple-element.23), channel_id=1, source_target_pairs={{0,2},{1,3},{2,0},{3,1},{4,6},{5,7},{6,4},{7,5},{8,10},{9,11},{10,... | collective-permute-start | bytes 393224 | tf_op jit(solution)/shard_map/ppermute | solution.py:23
  7.7 0.0 collective-permute-start.4
  7.7 1.3 %collective-permute-start.1 = (bf16[256,128]{1,0:T(8,128)(2,1)S(1)}, bf16[256,128]{1,0:T(8,128)(2,1)S(1)}, u32[]{:S(2)}, u32[]{:S(2)}) collective-permute-start(bf16[256,128]{1,0:T(8,128)(2,1)S(1)} %get-tuple-element.20), channel_id=1, source_target_pairs={{0,8},{8,16},{16,24},{1,9},{9,17},{17,25},{2,10},{10,18},{18,26},{... | collective-permute-start | bytes 196616 | tf_op jit(solution)/shard_map/ppermute | solution.py:295
  9.0 3.0 %collective-permute-start = (s32[16,128]{1,0:T(8,128)S(1)}, s32[16,128]{1,0:T(8,128)S(1)}, u32[]{:S(2)}, u32[]{:S(2)}) collective-permute-start(s32[16,128]{1,0:T(8,128)S(1)} %get-tuple-element.19.packed), channel_id=1, source_target_pairs={{0,4},{1,5},{2,6},{3,7},{4,0},{5,1},{6,2},{7,3},{8,12},{9,13},{10,... | collective-permute-start | bytes 24584 | tf_op jit(solution)/shard_map/ppermute | solution.py:23
  12.1 0.6 %choose.2.own = bf16[1024,1280]{1,0:T(8,128)(2,1)S(1)} custom-call(s32[16,128]{1,0:T(8,128)S(1)} %get-tuple-element.19.packed, bf16[2,128,128]{2,1,0:T(8,128)(2,1)S(1)} %bitcast.9), custom_call_target="tpu_custom_call" | custom-call | flops 1310720 | bytes 2621440 | tf_op jit(solution)/shard_map/choose/pallas_call | solution.py:175
  12.7 1.1 %collective-permute-done.packed = s32[16,128]{1,0:T(8,128)S(1)} collective-permute-done((s32[16,128]{1,0:T(8,128)S(1)}, s32[16,128]{1,0:T(8,128)S(1)}, u32[]{:S(2)}, u32[]{:S(2)}) %collective-permute-start) | collective-permute-done | bytes 8224 | tf_op jit(solution)/shard_map/ppermute | solution.py:23
  13.8 0.4 %choose.3.other = bf16[1024,1024]{1,0:T(8,128)(2,1)S(1)} custom-call(s32[16,128]{1,0:T(8,128)S(1)} %collective-permute-done.packed), custom_call_target="tpu_custom_call" | custom-call | flops 1048576 | bytes 2097152 | tf_op jit(solution)/shard_map/choose/pallas_call | solution.py:175
  14.2 0.0 collective-permute-done.2.refs_1_
  14.3 0.8 %place.3 = (bf16[256,128]{1,0:T(8,128)(2,1)S(1)}, bf16[256,128]{1,0:T(8,128)(2,1)S(1)}, bf16[256,128]{1,0:T(8,128)(2,1)S(1)}, bf16[256,128]{1,0:T(8,128)(2,1)S(1)}) custom-call(bf16[1024,1280]{1,0:T(8,128)(2,1)S(1)} %choose.2.own, bf16[1024,1024]{1,0:T(8,128)(2,1)S(1)} %choose.3.other, bf16[256,128]{1,0:T(8,128)(2,1)S(1)} %collective-permute-done.1.rim, ...), custom_call_target="tpu_custom_call" | custom-call | flops 335544320 | bytes 2621440 | tf_op jit(solution)/shard_map/place/pallas_call | solution.py:222
  15.1 3.9 %collective-permute-start.10 = (bf16[256,128]{1,0:T(8,128)(2,1)S(1)}, bf16[256,128]{1,0:T(8,128)(2,1)S(1)}, u32[]{:S(2)}, u32[]{:S(2)}) collective-permute-start(bf16[256,128]{1,0:T(8,128)(2,1)S(1)} %get-tuple-element.31), channel_id=1, source_target_pairs={{0,6},{1,7},{2,4},{3,5},{4,2},{5,3},{6,0},{7,1},{8,14},{9,15},{10,... | collective-permute-start | bytes 196616 | tf_op jit(solution)/shard_map/ppermute | solution.py:23
  19.0 1.2 %collective-permute-start.11 = (bf16[256,128]{1,0:T(8,128)(2,1)S(1)}, bf16[256,128]{1,0:T(8,128)(2,1)S(1)}, u32[]{:S(2)}, u32[]{:S(2)}) collective-permute-start(bf16[256,128]{1,0:T(8,128)(2,1)S(1)} %get-tuple-element.32), channel_id=1, source_target_pairs={{0,7},{1,6},{2,5},{3,4},{4,3},{5,2},{6,1},{7,0},{8,15},{9,14},{10,... | collective-permute-start | bytes 196616 | tf_op jit(solution)/shard_map/ppermute | solution.py:23
  20.2 0.8 %collective-permute-start.8 = (bf16[256,128]{1,0:T(8,128)(2,1)S(1)}, bf16[256,128]{1,0:T(8,128)(2,1)S(1)}, u32[]{:S(2)}, u32[]{:S(2)}) collective-permute-start(bf16[256,128]{1,0:T(8,128)(2,1)S(1)} %get-tuple-element.29), channel_id=1, source_target_pairs={{0,4},{1,5},{2,6},{3,7},{4,0},{5,1},{6,2},{7,3},{8,12},{9,13},{10,... | collective-permute-start | bytes 196616 | tf_op jit(solution)/shard_map/ppermute | solution.py:23
  21.0 1.9 %collective-permute-start.9 = (bf16[256,128]{1,0:T(8,128)(2,1)S(1)}, bf16[256,128]{1,0:T(8,128)(2,1)S(1)}, u32[]{:S(2)}, u32[]{:S(2)}) collective-permute-start(bf16[256,128]{1,0:T(8,128)(2,1)S(1)} %get-tuple-element.30), channel_id=1, source_target_pairs={{0,5},{1,4},{2,7},{3,6},{4,1},{5,0},{6,3},{7,2},{8,13},{9,12},{10,... | collective-permute-start | bytes 196616 | tf_op jit(solution)/shard_map/ppermute | solution.py:23
  22.9 0.8 %place.2 = (bf16[256,128]{1,0:T(8,128)(2,1)S(1)}, bf16[256,128]{1,0:T(8,128)(2,1)S(1)}, bf16[256,128]{1,0:T(8,128)(2,1)S(1)}, bf16[256,128]{1,0:T(8,128)(2,1)S(1)}) custom-call(bf16[1024,1280]{1,0:T(8,128)(2,1)S(1)} %choose.2.own, bf16[1024,1024]{1,0:T(8,128)(2,1)S(1)} %choose.3.other, bf16[256,128]{1,0:T(8,128)(2,1)S(1)} %collective-permute-done.1.rim, ...), custom_call_target="tpu_custom_call" | custom-call | flops 335544320 | bytes 2621440 | tf_op jit(solution)/shard_map/place/pallas_call | solution.py:222
  23.7 1.7 %collective-permute-start.5 = (bf16[256,128]{1,0:T(8,128)(2,1)S(1)}, bf16[256,128]{1,0:T(8,128)(2,1)S(1)}, u32[]{:S(2)}, u32[]{:S(2)}) collective-permute-start(bf16[256,128]{1,0:T(8,128)(2,1)S(1)} %get-tuple-element.26), channel_id=1, source_target_pairs={{0,1},{1,0},{2,3},{3,2},{4,5},{5,4},{6,7},{7,6},{8,9},{9,8},{10,11... | collective-permute-start | bytes 196616 | tf_op jit(solution)/shard_map/ppermute | solution.py:23
  25.5 1.2 %collective-permute-start.6 = (bf16[256,128]{1,0:T(8,128)(2,1)S(1)}, bf16[256,128]{1,0:T(8,128)(2,1)S(1)}, u32[]{:S(2)}, u32[]{:S(2)}) collective-permute-start(bf16[256,128]{1,0:T(8,128)(2,1)S(1)} %get-tuple-element.27), channel_id=1, source_target_pairs={{0,2},{1,3},{2,0},{3,1},{4,6},{5,7},{6,4},{7,5},{8,10},{9,11},{10,... | collective-permute-start | bytes 196616 | tf_op jit(solution)/shard_map/ppermute | solution.py:23
  26.7 0.1 collective-permute-done.11.refs_7_
  26.8 2.1 %collective-permute-start.7 = (bf16[256,128]{1,0:T(8,128)(2,1)S(1)}, bf16[256,128]{1,0:T(8,128)(2,1)S(1)}, u32[]{:S(2)}, u32[]{:S(2)}) collective-permute-start(bf16[256,128]{1,0:T(8,128)(2,1)S(1)} %get-tuple-element.28), channel_id=1, source_target_pairs={{0,3},{1,2},{2,1},{3,0},{4,7},{5,6},{6,5},{7,4},{8,11},{9,10},{10,... | collective-permute-start | bytes 196616 | tf_op jit(solution)/shard_map/ppermute | solution.py:23
  28.9 1.4 %collective-permute-done.8.refs_4_ = bf16[256,128]{1,0:T(8,128)(2,1)S(1)} collective-permute-done((bf16[256,128]{1,0:T(8,128)(2,1)S(1)}, bf16[256,128]{1,0:T(8,128)(2,1)S(1)}, u32[]{:S(2)}, u32[]{:S(2)}) %collective-permute-start.8) | collective-permute-done | bytes 65568 | tf_op jit(solution)/shard_map/ppermute | solution.py:23
  30.2 1.8 %collective-permute-done.9.refs_5_ = bf16[256,128]{1,0:T(8,128)(2,1)S(1)} collective-permute-done((bf16[256,128]{1,0:T(8,128)(2,1)S(1)}, bf16[256,128]{1,0:T(8,128)(2,1)S(1)}, u32[]{:S(2)}, u32[]{:S(2)}) %collective-permute-start.9) | collective-permute-done | bytes 65568 | tf_op jit(solution)/shard_map/ppermute | solution.py:23
  32.1 1.4 %collective-permute-done.7.refs_3_ = bf16[256,128]{1,0:T(8,128)(2,1)S(1)} collective-permute-done((bf16[256,128]{1,0:T(8,128)(2,1)S(1)}, bf16[256,128]{1,0:T(8,128)(2,1)S(1)}, u32[]{:S(2)}, u32[]{:S(2)}) %collective-permute-start.7) | collective-permute-done | bytes 65568 | tf_op jit(solution)/shard_map/ppermute | solution.py:23
  33.5 0.8 %join.1 = bf16[1024,128]{1,0:T(8,128)(2,1)} custom-call(bf16[256,128]{1,0:T(8,128)(2,1)S(1)} %get-tuple-element.25.refs_0_, bf16[256,128]{1,0:T(8,128)(2,1)S(1)} %collective-permute-done.5.refs_1_, bf16[256,128]{1,0:T(8,128)(2,1)S(1)} %collective-permute-done.6.refs_2_, bf16[256,128]{1,0:T(8,128)(2,1)S(1)} %collective-permute-done.7.refs_3_, ...), custom_call_target="tpu_custom_call" | custom-call | tf_op jit(solution)/shard_map/join/pallas_call | solution.py:258
  (8 shorter events, 0.0 us)
Async XLA Ops:
  0.0 12.1 %copy-start = (bf16[1,1,2,128,128]{4,3,2,1,0:T(8,128)(2,1)S(1)}, bf16[1,1,2,128,128]{4,3,2,1,0:T(8,128)(2,1)}, u32[]{:S(2)}) copy-start(bf16[1,1,2,128,128]{4,3,2,1,0:T(8,128)(2,1)} %param.14) | copy-start | bytes 196612
  3.1 11.2 %collective-permute-start.2 = (bf16[512,128]{1,0:T(8,128)(2,1)S(1)}, bf16[512,128]{1,0:T(8,128)(2,1)S(1)}, u32[]{:S(2)}, u32[]{:S(2)}) collective-permute-start(bf16[512,128]{1,0:T(8,128)(2,1)S(1)} %get-tuple-element.22), channel_id=1, source_target_pairs={{0,1},{1,0},{2,3},{3,2},{4,5},{5,4},{6,7},{7,6},{8,9},{9,8},{10,11... | collective-permute-start | bytes 393224 | tf_op jit(solution)/shard_map/ppermute | solution.py:23
  6.1 8.1 %collective-permute-start.3 = (bf16[512,128]{1,0:T(8,128)(2,1)S(1)}, bf16[512,128]{1,0:T(8,128)(2,1)S(1)}, u32[]{:S(2)}, u32[]{:S(2)}) collective-permute-start(bf16[512,128]{1,0:T(8,128)(2,1)S(1)} %get-tuple-element.23), channel_id=1, source_target_pairs={{0,2},{1,3},{2,0},{3,1},{4,6},{5,7},{6,4},{7,5},{8,10},{9,11},{10,... | collective-permute-start | bytes 393224 | tf_op jit(solution)/shard_map/ppermute | solution.py:23
  7.7 6.5 %collective-permute-start.4 = (bf16[512,128]{1,0:T(8,128)(2,1)S(1)}, bf16[512,128]{1,0:T(8,128)(2,1)S(1)}, u32[]{:S(2)}, u32[]{:S(2)}) collective-permute-start(bf16[512,128]{1,0:T(8,128)(2,1)S(1)} %get-tuple-element.24), channel_id=1, source_target_pairs={{0,3},{1,2},{2,1},{3,0},{4,7},{5,6},{6,5},{7,4},{8,11},{9,10},{10,... | collective-permute-start | bytes 393224 | tf_op jit(solution)/shard_map/ppermute | solution.py:23
  7.7 6.5 %collective-permute-start.1 = (bf16[256,128]{1,0:T(8,128)(2,1)S(1)}, bf16[256,128]{1,0:T(8,128)(2,1)S(1)}, u32[]{:S(2)}, u32[]{:S(2)}) collective-permute-start(bf16[256,128]{1,0:T(8,128)(2,1)S(1)} %get-tuple-element.20), channel_id=1, source_target_pairs={{0,8},{8,16},{16,24},{1,9},{9,17},{17,25},{2,10},{10,18},{18,26},{... | collective-permute-start | bytes 196616 | tf_op jit(solution)/shard_map/ppermute | solution.py:295
  9.0 4.8 %collective-permute-start = (s32[16,128]{1,0:T(8,128)S(1)}, s32[16,128]{1,0:T(8,128)S(1)}, u32[]{:S(2)}, u32[]{:S(2)}) collective-permute-start(s32[16,128]{1,0:T(8,128)S(1)} %get-tuple-element.19.packed), channel_id=1, source_target_pairs={{0,4},{1,5},{2,6},{3,7},{4,0},{5,1},{6,2},{7,3},{8,12},{9,13},{10,... | collective-permute-start | bytes 24584 | tf_op jit(solution)/shard_map/ppermute | solution.py:23
  15.1 10.4 %collective-permute-start.10 = (bf16[256,128]{1,0:T(8,128)(2,1)S(1)}, bf16[256,128]{1,0:T(8,128)(2,1)S(1)}, u32[]{:S(2)}, u32[]{:S(2)}) collective-permute-start(bf16[256,128]{1,0:T(8,128)(2,1)S(1)} %get-tuple-element.31), channel_id=1, source_target_pairs={{0,6},{1,7},{2,4},{3,5},{4,2},{5,3},{6,0},{7,1},{8,14},{9,15},{10,... | collective-permute-start | bytes 196616 | tf_op jit(solution)/shard_map/ppermute | solution.py:23
  19.0 7.8 %collective-permute-start.11 = (bf16[256,128]{1,0:T(8,128)(2,1)S(1)}, bf16[256,128]{1,0:T(8,128)(2,1)S(1)}, u32[]{:S(2)}, u32[]{:S(2)}) collective-permute-start(bf16[256,128]{1,0:T(8,128)(2,1)S(1)} %get-tuple-element.32), channel_id=1, source_target_pairs={{0,7},{1,6},{2,5},{3,4},{4,3},{5,2},{6,1},{7,0},{8,15},{9,14},{10,... | collective-permute-start | bytes 196616 | tf_op jit(solution)/shard_map/ppermute | solution.py:23
  20.2 10.1 %collective-permute-start.8 = (bf16[256,128]{1,0:T(8,128)(2,1)S(1)}, bf16[256,128]{1,0:T(8,128)(2,1)S(1)}, u32[]{:S(2)}, u32[]{:S(2)}) collective-permute-start(bf16[256,128]{1,0:T(8,128)(2,1)S(1)} %get-tuple-element.29), channel_id=1, source_target_pairs={{0,4},{1,5},{2,6},{3,7},{4,0},{5,1},{6,2},{7,3},{8,12},{9,13},{10,... | collective-permute-start | bytes 196616 | tf_op jit(solution)/shard_map/ppermute | solution.py:23
  21.0 11.1 %collective-permute-start.9 = (bf16[256,128]{1,0:T(8,128)(2,1)S(1)}, bf16[256,128]{1,0:T(8,128)(2,1)S(1)}, u32[]{:S(2)}, u32[]{:S(2)}) collective-permute-start(bf16[256,128]{1,0:T(8,128)(2,1)S(1)} %get-tuple-element.30), channel_id=1, source_target_pairs={{0,5},{1,4},{2,7},{3,6},{4,1},{5,0},{6,3},{7,2},{8,13},{9,12},{10,... | collective-permute-start | bytes 196616 | tf_op jit(solution)/shard_map/ppermute | solution.py:23
  23.7 8.3 %collective-permute-start.5 = (bf16[256,128]{1,0:T(8,128)(2,1)S(1)}, bf16[256,128]{1,0:T(8,128)(2,1)S(1)}, u32[]{:S(2)}, u32[]{:S(2)}) collective-permute-start(bf16[256,128]{1,0:T(8,128)(2,1)S(1)} %get-tuple-element.26), channel_id=1, source_target_pairs={{0,1},{1,0},{2,3},{3,2},{4,5},{5,4},{6,7},{7,6},{8,9},{9,8},{10,11... | collective-permute-start | bytes 196616 | tf_op jit(solution)/shard_map/ppermute | solution.py:23
  25.5 6.6 %collective-permute-start.6 = (bf16[256,128]{1,0:T(8,128)(2,1)S(1)}, bf16[256,128]{1,0:T(8,128)(2,1)S(1)}, u32[]{:S(2)}, u32[]{:S(2)}) collective-permute-start(bf16[256,128]{1,0:T(8,128)(2,1)S(1)} %get-tuple-element.27), channel_id=1, source_target_pairs={{0,2},{1,3},{2,0},{3,1},{4,6},{5,7},{6,4},{7,5},{8,10},{9,11},{10,... | collective-permute-start | bytes 196616 | tf_op jit(solution)/shard_map/ppermute | solution.py:23
  26.8 6.7 %collective-permute-start.7 = (bf16[256,128]{1,0:T(8,128)(2,1)S(1)}, bf16[256,128]{1,0:T(8,128)(2,1)S(1)}, u32[]{:S(2)}, u32[]{:S(2)}) collective-permute-start(bf16[256,128]{1,0:T(8,128)(2,1)S(1)} %get-tuple-element.28), channel_id=1, source_target_pairs={{0,3},{1,2},{2,1},{3,0},{4,7},{5,6},{6,5},{7,4},{8,11},{9,10},{10,... | collective-permute-start | bytes 196616 | tf_op jit(solution)/shard_map/ppermute | solution.py:23
